TPU v7x, 32 devices: a whole 2x2x4 slice. The times are simulated.
32 devices in a mesh: slab: 2 (over y), pencil: 16 (over z, x, core).
Axes of the slice: x: 2, y: 2, z: 4, core: 2. Of those that a mesh axis runs over, the one named last changes fastest.
Arguments:
- concentration: float32 [512, 512, 256], P('slab', 'pencil'), may hold values from -2 to 2.8
Outputs:
- updated: float32 [512, 512, 256], P('slab', 'pencil')
- mass: float32 [], replicated
All inputs are finite; a program needn't handle non-finite values.
Results may differ from a plain program's by a relative error of at most 0.0002.
Values sent between devices are 32-bit elements; how exact they have to be, the bound alone decides.
No kernel may reach another device: no remote copies, remote signals or barrier semaphores. Data moves between devices by JAX's collectives and lax.ppermute only.
A program may use at most 128 MiB of HBM per device.

v0:
```python
import math

import jax
import jax.numpy as jnp
from jax import lax
from jax.sharding import PartitionSpec as P

NX = 512
NY = 512
NZ = 256


time_step = 1.0
stiffness = 1.0


def twiddle_tables(length):
    index = jnp.arange(length, dtype=jnp.int32)
    product = index[:, None] * index[None, :] % length
    angle = 2.0 * math.pi / length * product.astype(jnp.float32)
    return (jnp.cos(angle), jnp.sin(angle))


def wavenumber(index, length):
    signed = jnp.where(index < length // 2, index, index - length)
    return 2.0 * math.pi / length * signed.astype(jnp.float32)


def last_forward(field, cosines, sines):
    length = field.shape[-1]
    flat = field.reshape(-1, length)
    real_part = jnp.dot(flat, cosines, precision=lax.Precision.HIGHEST)
    imag_part = -jnp.dot(flat, sines, precision=lax.Precision.HIGHEST)
    shape = field.shape[:-1] + (cosines.shape[1],)
    return (real_part.reshape(shape), imag_part.reshape(shape))


def last_inverse_real(real_part, imag_part, cosines, sines):
    length = real_part.shape[-1]
    flat_real = real_part.reshape(-1, length)
    flat_imag = imag_part.reshape(-1, length)
    result = jnp.dot(flat_real, cosines, precision=lax.Precision.HIGHEST) - jnp.dot(
        flat_imag, sines, precision=lax.Precision.HIGHEST
    )
    return result.reshape(real_part.shape[:-1] + (cosines.shape[1],))


def transform_axis(real_part, imag_part, cosines, sines, form, inverse):
    cos_real = jnp.einsum(form, cosines, real_part, precision=lax.Precision.HIGHEST)
    cos_imag = jnp.einsum(form, cosines, imag_part, precision=lax.Precision.HIGHEST)
    sin_real = jnp.einsum(form, sines, real_part, precision=lax.Precision.HIGHEST)
    sin_imag = jnp.einsum(form, sines, imag_part, precision=lax.Precision.HIGHEST)
    if inverse:
        return (cos_real - sin_imag, cos_imag + sin_real)
    return (cos_real + sin_imag, cos_imag - sin_real)


def local(concentration):
    cube = concentration * concentration * concentration
    depth_cos, depth_sin = twiddle_tables(NZ)
    column_cos, column_sin = twiddle_tables(NY)
    row_cos, row_sin = twiddle_tables(NX)
    columns_kept = NZ // 2
    forward_cos = depth_cos[:, :columns_kept]
    forward_sin = depth_sin[:, :columns_kept]
    weights = jnp.where(jnp.arange(columns_kept, dtype=jnp.int32) == 0, 1.0, 2.0).astype(
        jnp.float32
    )
    inverse_cos = weights[:, None] * depth_cos[:columns_kept, :]
    inverse_sin = weights[:, None] * depth_sin[:columns_kept, :]
    conc_real, conc_imag = last_forward(concentration, forward_cos, forward_sin)
    cube_real, cube_imag = last_forward(cube, forward_cos, forward_sin)
    parts = (
        lax.all_to_all(conc_real, "pencil", split_axis=0, concat_axis=1, tiled=True),
        lax.all_to_all(conc_imag, "pencil", split_axis=0, concat_axis=1, tiled=True),
        lax.all_to_all(cube_real, "pencil", split_axis=0, concat_axis=1, tiled=True),
        lax.all_to_all(cube_imag, "pencil", split_axis=0, concat_axis=1, tiled=True),
    )
    fields = transform_axis(
        parts[0], parts[1], column_cos, column_sin, "ky,ayz->akz", False
    ) + transform_axis(parts[2], parts[3], column_cos, column_sin, "ky,ayz->akz", False)
    parts = (
        lax.all_to_all(fields[0], ("slab", "pencil"), split_axis=1, concat_axis=0, tiled=True),
        lax.all_to_all(fields[1], ("slab", "pencil"), split_axis=1, concat_axis=0, tiled=True),
        lax.all_to_all(fields[2], ("slab", "pencil"), split_axis=1, concat_axis=0, tiled=True),
        lax.all_to_all(fields[3], ("slab", "pencil"), split_axis=1, concat_axis=0, tiled=True),
    )
    spectra = transform_axis(
        parts[0], parts[1], row_cos, row_sin, "kx,xyz->kyz", False
    ) + transform_axis(parts[2], parts[3], row_cos, row_sin, "kx,xyz->kyz", False)
    conc_real, conc_imag, cube_real, cube_imag = spectra
    local_rows = conc_real.shape[1]
    offset = lax.axis_index(("slab", "pencil")) * local_rows
    depth_index = jnp.arange(columns_kept, dtype=jnp.int32)
    wave_first = wavenumber(jnp.arange(NX, dtype=jnp.int32), NX)
    wave_second = wavenumber(offset + jnp.arange(local_rows, dtype=jnp.int32), NY)
    wave_third = wavenumber(depth_index, NZ)
    wave_square = (
        wave_first[:, None, None] ** 2
        + wave_second[None, :, None] ** 2
        + wave_third[None, None, :] ** 2
    )
    keep = jnp.where(depth_index == NZ // 2, 0.0, 1.0).astype(jnp.float32)[None, None, :]
    divisor = 1.0 + time_step * stiffness * wave_square * wave_square
    retain = keep * (1.0 + time_step * wave_square) / divisor
    forcing = keep * (time_step * wave_square) / divisor
    next_real = retain * conc_real - forcing * cube_real
    next_imag = retain * conc_imag - forcing * cube_imag
    back_real, back_imag = transform_axis(
        next_real, next_imag, row_cos, row_sin, "kx,xyz->kyz", True
    )
    parts = (
        lax.all_to_all(back_real, ("slab", "pencil"), split_axis=0, concat_axis=1, tiled=True),
        lax.all_to_all(back_imag, ("slab", "pencil"), split_axis=0, concat_axis=1, tiled=True),
    )
    columns = transform_axis(parts[0], parts[1], column_cos, column_sin, "ky,ayz->akz", True)
    scale = 1.0 / (NX * NY * NZ)
    home = (
        lax.all_to_all(columns[0], "pencil", split_axis=1, concat_axis=0, tiled=True),
        lax.all_to_all(columns[1], "pencil", split_axis=1, concat_axis=0, tiled=True),
    )
    updated = last_inverse_real(home[0], home[1], inverse_cos, inverse_sin) * scale
    mass = lax.psum(jnp.sum(concentration), ("slab", "pencil")) / (NX * NY * NZ)
    return (updated, mass)


def solution(mesh):
    return jax.shard_map(
        local,
        mesh=mesh,
        in_specs=(P("slab", "pencil", None),),
        out_specs=(P("slab", "pencil", None), P()),
        check_vma=False,
    )
```

profile of v0, /device:TPU:0, one launch (start us, length us, event | category | flops | bytes accessed | tf_op | source)
XLA Modules:
  0.0 1350.7 jit_solution(16831538249325290632)
XLA Ops:
  1.6 14.3 %convolution_bitcast_fusion = f32[8192,128]{0,1:T(8,128)} fusion(f32[8192,256]{1,0:T(8,128)} %bitcast.152, f32[256,256]{1,0:T(8,128)S(1)} %fusion.86), kind=kOutput, calls=%fused_computation.6 | convolution fusion | flops 3221225472 | bytes 12713984 | tf_op jit(solution)/shard_map/dot_general | solution.py:32
  30.2 14.3 %fusion.1 = f32[8192,128]{0,1:T(8,128)} fusion(f32[8192,256]{1,0:T(8,128)} %bitcast.153, f32[256,256]{1,0:T(8,128)S(1)} %fusion.85), kind=kOutput, calls=%fused_computation.5 | convolution fusion | flops 3222274048 | bytes 12713984 | tf_op jit(solution)/shard_map/dot_general | solution.py:33
  50.2 56.6 %all-to-all-done = f32[256,32,128]{2,1,0:T(8,128)} async-done(((f32[256,32,128]{2,1,0:T(8,128)}), f32[256,32,128]{2,1,0:T(8,128)}, u32[]{:S(2)}, u32[]{:S(2)}) %all-to-all-start) | async-done | bytes 4194336 | tf_op jit(solution)/shard_map/all_to_all | solution.py:74
  106.8 20.1 %all-to-all-start.1 = ((f32[256,32,128]{2,1,0:T(8,128)}), f32[256,32,128]{2,1,0:T(8,128)}, u32[]{:S(2)}, u32[]{:S(2)}) async-start(f32[256,32,128]{2,1,0:T(8,128)} %bitcast.177), calls=%async_computation.1 | async-start | bytes 8388608 | tf_op jit(solution)/shard_map/all_to_all | solution.py:75
  141.3 63.1 %all-to-all-done.1 = f32[256,32,128]{2,1,0:T(8,128)} async-done(((f32[256,32,128]{2,1,0:T(8,128)}), f32[256,32,128]{2,1,0:T(8,128)}, u32[]{:S(2)}, u32[]{:S(2)}) %all-to-all-start.1) | async-done | bytes 4194336 | tf_op jit(solution)/shard_map/all_to_all | solution.py:75
  204.4 19.7 %all-to-all-start.5 = ((f32[256,32,128]{2,1,0:T(8,128)}), f32[256,32,128]{2,1,0:T(8,128)}, u32[]{:S(2)}, u32[]{:S(2)}) async-start(f32[256,32,128]{2,1,0:T(8,128)} %bitcast.171), calls=%async_computation.5 | async-start | bytes 8388608 | tf_op jit(solution)/shard_map/all_to_all | solution.py:77
  234.5 67.1 %all-to-all-done.5 = f32[256,32,128]{2,1,0:T(8,128)} async-done(((f32[256,32,128]{2,1,0:T(8,128)}), f32[256,32,128]{2,1,0:T(8,128)}, u32[]{:S(2)}, u32[]{:S(2)}) %all-to-all-start.5) | async-done | bytes 4194336 | tf_op jit(solution)/shard_map/all_to_all | solution.py:77
  301.7 19.9 %all-to-all-start.4 = ((f32[256,32,128]{2,1,0:T(8,128)}), f32[256,32,128]{2,1,0:T(8,128)}, u32[]{:S(2)}, u32[]{:S(2)}) async-start(f32[256,32,128]{2,1,0:T(8,128)} %fusion.83), calls=%async_computation.4 | async-start | bytes 8388608 | tf_op jit(solution)/shard_map/all_to_all | solution.py:76
  328.7 17.0 %fusion.45 = f32[16,128,512]{2,1,0:T(8,128)S(1)} fusion(f32[16,512,128]{2,1,0:T(8,128)S(1)} %bitcast.159), kind=kOutput, calls=%fused_computation.66 | convolution fusion | flops 6446120960 | bytes 8388608 | tf_op jit(solution)/shard_map/ky,ayz->akz/dot_general | solution.py:49
  345.7 19.2 %add_bitcast_fusion.2 = f32[16,512,128]{1,2,0:T(8,128)} fusion(f32[16,128,512]{2,1,0:T(8,128)S(1)} %fusion.45, f32[16,512,128]{2,1,0:T(8,128)S(1)} %bitcast.165), kind=kOutput, calls=%fused_computation.21 | convolution fusion | flops 6447169536 | bytes 12582912 | tf_op jit(solution)/shard_map/ky,ayz->akz/dot_general | solution.py:52
  370.4 28.5 %all-to-all-done.4 = f32[256,32,128]{2,1,0:T(8,128)} async-done(((f32[256,32,128]{2,1,0:T(8,128)}), f32[256,32,128]{2,1,0:T(8,128)}, u32[]{:S(2)}, u32[]{:S(2)}) %all-to-all-start.4) | async-done | bytes 4194336 | tf_op jit(solution)/shard_map/all_to_all | solution.py:76
  398.9 19.9 %all-to-all-start.2 = ((f32[16,512,128]{2,0,1:T(8,128)}), f32[16,512,128]{2,0,1:T(8,128)}, u32[]{:S(2)}, u32[]{:S(2)}) async-start(f32[16,512,128]{2,0,1:T(8,128)} %copy.124), calls=%async_computation.2 | async-start | bytes 8388608 | tf_op jit(solution)/shard_map/all_to_all | solution.py:83
  418.8 19.5 %fusion.41 = f32[16,128,512]{2,1,0:T(8,128)S(1)} fusion(f32[16,512,128]{2,1,0:T(8,128)} %bitcast.166), kind=kOutput, calls=%fused_computation.62 | convolution fusion | flops 6446120960 | bytes 8388608 | tf_op jit(solution)/shard_map/ky,ayz->akz/dot_general | solution.py:50
  438.4 18.3 %subtract_bitcast_fusion.2 = f32[16,512,128]{1,2,0:T(8,128)} fusion(f32[16,128,512]{2,1,0:T(8,128)S(1)} %fusion.41, f32[16,512,128]{2,1,0:T(8,128)S(1)} %bitcast.160), kind=kOutput, calls=%fused_computation.20 | convolution fusion | flops 6447169536 | bytes 12582912 | tf_op jit(solution)/shard_map/ky,ayz->akz/dot_general | solution.py:51
  462.1 51.6 %all-to-all-done.2 = f32[16,512,128]{2,0,1:T(8,128)} async-done(((f32[16,512,128]{2,0,1:T(8,128)}), f32[16,512,128]{2,0,1:T(8,128)}, u32[]{:S(2)}, u32[]{:S(2)}) %all-to-all-start.2) | async-done | bytes 4194336 | tf_op jit(solution)/shard_map/all_to_all | solution.py:83
  524.7 17.0 %fusion.35 = f32[16,128,512]{2,1,0:T(8,128)S(1)} fusion(f32[16,512,128]{2,1,0:T(8,128)S(1)} %bitcast.161), kind=kOutput, calls=%fused_computation.56 | convolution fusion | flops 6446120960 | bytes 8388608 | tf_op jit(solution)/shard_map/ky,ayz->akz/dot_general | solution.py:50
  541.7 19.3 %subtract_bitcast_fusion.1 = f32[16,512,128]{1,2,0:T(8,128)} fusion(f32[16,128,512]{2,1,0:T(8,128)S(1)} %fusion.35, f32[16,512,128]{2,1,0:T(8,128)S(1)} %bitcast.167), kind=kOutput, calls=%fused_computation.18 | convolution fusion | flops 6447169536 | bytes 12582912 | tf_op jit(solution)/shard_map/ky,ayz->akz/dot_general | solution.py:51
  566.5 45.9 %all-to-all-done.3 = f32[16,512,128]{2,0,1:T(8,128)} async-done(((f32[16,512,128]{2,0,1:T(8,128)}), f32[16,512,128]{2,0,1:T(8,128)}, u32[]{:S(2)}, u32[]{:S(2)}) %all-to-all-start.3) | async-done | bytes 4194336 | tf_op jit(solution)/shard_map/all_to_all | solution.py:84
  616.2 19.3 %fusion.39 = f32[16,128,512]{2,1,0:T(8,128)S(1)} fusion(f32[16,512,128]{2,1,0:T(8,128)} %bitcast.168), kind=kOutput, calls=%fused_computation.60 | convolution fusion | flops 6446120960 | bytes 8388608 | tf_op jit(solution)/shard_map/ky,ayz->akz/dot_general | solution.py:49
  635.5 18.3 %add_bitcast_fusion.1 = f32[16,512,128]{1,2,0:T(8,128)} fusion(f32[16,128,512]{2,1,0:T(8,128)S(1)} %fusion.39, f32[16,512,128]{2,1,0:T(8,128)S(1)} %bitcast.162), kind=kOutput, calls=%fused_computation.19 | convolution fusion | flops 6447169536 | bytes 12582912 | tf_op jit(solution)/shard_map/ky,ayz->akz/dot_general | solution.py:52
  659.4 51.7 %all-to-all-done.7 = f32[16,512,128]{2,0,1:T(8,128)} async-done(((f32[16,512,128]{2,0,1:T(8,128)}), f32[16,512,128]{2,0,1:T(8,128)}, u32[]{:S(2)}, u32[]{:S(2)}) %all-to-all-start.7) | async-done | bytes 4194336 | tf_op jit(solution)/shard_map/all_to_all | solution.py:86
  789.7 20.5 %all-to-all-done.6 = f32[16,512,128]{2,0,1:T(8,128)} async-done(((f32[16,512,128]{2,0,1:T(8,128)}), f32[16,512,128]{2,0,1:T(8,128)}, u32[]{:S(2)}, u32[]{:S(2)}) %all-to-all-start.6) | async-done | bytes 4194336 | tf_op jit(solution)/shard_map/all_to_all | solution.py:85
  850.7 14.8 %multiply_subtract_fusion.1 = f32[512,16,128]{2,0,1:T(8,128)S(1)} fusion(f32[512,16,128]{2,0,1:T(8,128)} %fusion.37, f32[512,16,128]{2,0,1:T(8,128)S(1)} %copy-done.17, f32[512,16,128]{2,0,1:T(8,128)S(1)} %copy-done.16, f32[512,16,128]{2,0,1:T(8,128)S(1)} %bitcast.173, f32[128]{0:T(128)S(1)} %get-tuple-element.5, f32[512,16]{0,1:T(8,128)S(1)} %broadcast_add_fusion, ...), kind=kOutput, calls=%fused_computation.17 | convolution fusion | flops 6459752448 | bytes 21005312 | tf_op jit(solution)/shard_map/kx,xyz->kyz/dot_general | solution.py:52
  913.1 66.9 %all-to-all-done.9 = f32[512,16,128]{2,1,0:T(8,128)} async-done(((f32[512,16,128]{2,1,0:T(8,128)}), f32[512,16,128]{2,1,0:T(8,128)}, u32[]{:S(2)}, u32[]{:S(2)}) %all-to-all-start.9) | async-done | bytes 4194336 | tf_op jit(solution)/shard_map/all_to_all | solution.py:114
  988.4 18.3 %fusion.23 = f32[16,128,512]{2,1,0:T(8,128)} fusion(f32[16,512,128]{2,1,0:T(8,128)S(1)} %bitcast.163), kind=kOutput, calls=%fused_computation.44 | convolution fusion | flops 6446120960 | bytes 8388608 | tf_op jit(solution)/shard_map/ky,ayz->akz/dot_general | solution.py:50
  1006.6 72.2 %all-to-all-done.8 = f32[512,16,128]{2,1,0:T(8,128)} async-done(((f32[512,16,128]{2,1,0:T(8,128)}), f32[512,16,128]{2,1,0:T(8,128)}, u32[]{:S(2)}, u32[]{:S(2)}) %all-to-all-start.8) | async-done | bytes 4194336 | tf_op jit(solution)/shard_map/all_to_all | solution.py:113
  1083.6 18.9 %add_bitcast_fusion = f32[16,512,128]{1,2,0:T(8,128)} fusion(f32[16,128,512]{2,1,0:T(8,128)S(1)} %copy-done.14, f32[16,512,128]{2,1,0:T(8,128)S(1)} %bitcast.169), kind=kOutput, calls=%fused_computation.14 | convolution fusion | flops 6447169536 | bytes 12582912 | tf_op jit(solution)/shard_map/ky,ayz->akz/dot_general | solution.py:51
  1112.7 19.5 %fusion.27 = f32[16,128,512]{2,1,0:T(8,128)S(1)} fusion(f32[16,512,128]{2,1,0:T(8,128)} %bitcast.170), kind=kOutput, calls=%fused_computation.48 | convolution fusion | flops 6446120960 | bytes 8388608 | tf_op jit(solution)/shard_map/ky,ayz->akz/dot_general | solution.py:49
  1132.3 18.3 %subtract_bitcast_fusion = f32[16,512,128]{1,2,0:T(8,128)} fusion(f32[16,128,512]{2,1,0:T(8,128)S(1)} %fusion.27, f32[16,512,128]{2,1,0:T(8,128)S(1)} %bitcast.164), kind=kOutput, calls=%fused_computation.15 | convolution fusion | flops 6447169536 | bytes 12582912 | tf_op jit(solution)/shard_map/ky,ayz->akz/dot_general | solution.py:52
  1156.0 34.0 %all-to-all-done.11 = f32[16,512,128]{2,0,1:T(8,128)} async-done(((f32[16,512,128]{2,0,1:T(8,128)}), f32[16,512,128]{2,0,1:T(8,128)}, u32[]{:S(2)}, u32[]{:S(2)}) %all-to-all-start.11) | async-done | bytes 4194336 | tf_op jit(solution)/shard_map/all_to_all | solution.py:120
  1190.0 19.7 %all-to-all-start.10 = ((f32[16,512,128]{2,0,1:T(8,128)}), f32[16,512,128]{2,0,1:T(8,128)}, u32[]{:S(2)}, u32[]{:S(2)}) async-start(f32[16,512,128]{2,0,1:T(8,128)} %copy.152), calls=%async_computation.10 | async-start | bytes 8388608 | tf_op jit(solution)/shard_map/all_to_all | solution.py:119
  1209.7 113.2 %psum.7 = f32[]{:T(128)} all-reduce(f32[]{:T(128)} %get-tuple-element.2), channel_id=1, replica_groups=mesh['slab'=2,'pencil'=16] {'slab','pencil'}, use_global_device_ids=true, to_apply=%region_1.2 | all-reduce | flops 1 | bytes 8 | tf_op jit(solution)/shard_map/psum | solution.py:123
  (103 shorter events, 310.3 us)
Async XLA Ops:
  1.6 222.5 %copy-start.21 = (f32[256,256]{1,0:T(8,128)}, f32[256,256]{1,0:T(8,128)S(1)}, u32[]{:S(2)}) copy-start(f32[256,256]{1,0:T(8,128)S(1)} %fusion.86) | copy-start | bytes 786436
  21.6 85.2 %all-to-all-start = ((f32[256,32,128]{2,1,0:T(8,128)}), f32[256,32,128]{2,1,0:T(8,128)}, u32[]{:S(2)}, u32[]{:S(2)}) async-start(f32[256,32,128]{2,1,0:T(8,128)} %bitcast.178), calls=%async_computation | async-start | bytes 8388608 | tf_op jit(solution)/shard_map/all_to_all | solution.py:74
  30.2 102.8 %copy-start.23 = (f32[256,256]{1,0:T(8,128)}, f32[256,256]{1,0:T(8,128)S(1)}, u32[]{:S(2)}) copy-start(f32[256,256]{1,0:T(8,128)S(1)} %fusion.85) | copy-start | bytes 786436
  106.8 97.6 %all-to-all-start.1 = ((f32[256,32,128]{2,1,0:T(8,128)}), f32[256,32,128]{2,1,0:T(8,128)}, u32[]{:S(2)}, u32[]{:S(2)}) async-start(f32[256,32,128]{2,1,0:T(8,128)} %bitcast.177), calls=%async_computation.1 | async-start | bytes 8388608 | tf_op jit(solution)/shard_map/all_to_all | solution.py:75
  204.4 97.2 %all-to-all-start.5 = ((f32[256,32,128]{2,1,0:T(8,128)}), f32[256,32,128]{2,1,0:T(8,128)}, u32[]{:S(2)}, u32[]{:S(2)}) async-start(f32[256,32,128]{2,1,0:T(8,128)} %bitcast.171), calls=%async_computation.5 | async-start | bytes 8388608 | tf_op jit(solution)/shard_map/all_to_all | solution.py:77
  301.7 97.2 %all-to-all-start.4 = ((f32[256,32,128]{2,1,0:T(8,128)}), f32[256,32,128]{2,1,0:T(8,128)}, u32[]{:S(2)}, u32[]{:S(2)}) async-start(f32[256,32,128]{2,1,0:T(8,128)} %fusion.83), calls=%async_computation.4 | async-start | bytes 8388608 | tf_op jit(solution)/shard_map/all_to_all | solution.py:76
  328.7 17.0 %copy-start.9 = (f32[16,16,32,128]{3,2,0,1:T(8,128)}, f32[16,16,32,128]{3,2,0,1:T(8,128)S(1)}, u32[]{:S(2)}) copy-start(f32[16,16,32,128]{3,2,0,1:T(8,128)S(1)} %copy.122) | copy-start | bytes 12582916
  398.9 114.8 %all-to-all-start.2 = ((f32[16,512,128]{2,0,1:T(8,128)}), f32[16,512,128]{2,0,1:T(8,128)}, u32[]{:S(2)}, u32[]{:S(2)}) async-start(f32[16,512,128]{2,0,1:T(8,128)} %copy.124), calls=%async_computation.2 | async-start | bytes 8388608 | tf_op jit(solution)/shard_map/all_to_all | solution.py:83
  418.8 19.6 %copy-start.4 = (f32[16,16,32,128]{3,2,0,1:T(8,128)S(1)}, f32[16,16,32,128]{3,2,0,1:T(8,128)}, u32[]{:S(2)}) copy-start(f32[16,16,32,128]{3,2,0,1:T(8,128)} %copy-done.3) | copy-start | bytes 12582916
  513.7 98.7 %all-to-all-start.3 = ((f32[16,512,128]{2,0,1:T(8,128)}), f32[16,512,128]{2,0,1:T(8,128)}, u32[]{:S(2)}, u32[]{:S(2)}) async-start(f32[16,512,128]{2,0,1:T(8,128)} %copy.129), calls=%async_computation.3 | async-start | bytes 8388608 | tf_op jit(solution)/shard_map/all_to_all | solution.py:84
  524.7 17.0 %copy-start.10 = (f32[16,16,32,128]{3,2,1,0:T(8,128)}, f32[16,16,32,128]{3,2,1,0:T(8,128)S(1)}, u32[]{:S(2)}) copy-start(f32[16,16,32,128]{3,2,1,0:T(8,128)S(1)} %copy.134) | copy-start | bytes 12582916
  612.4 98.7 %all-to-all-start.7 = ((f32[16,512,128]{2,0,1:T(8,128)}), f32[16,512,128]{2,0,1:T(8,128)}, u32[]{:S(2)}, u32[]{:S(2)}) async-start(f32[16,512,128]{2,0,1:T(8,128)} %copy.143), calls=%async_computation.7 | async-start | bytes 8388608 | tf_op jit(solution)/shard_map/all_to_all | solution.py:86
  616.2 19.4 %copy-start.6 = (f32[16,16,32,128]{3,2,1,0:T(8,128)S(1)}, f32[16,16,32,128]{3,2,1,0:T(8,128)}, u32[]{:S(2)}) copy-start(f32[16,16,32,128]{3,2,1,0:T(8,128)} %copy-done.5) | copy-start | bytes 12582916
  711.1 99.1 %all-to-all-start.6 = ((f32[16,512,128]{2,0,1:T(8,128)}), f32[16,512,128]{2,0,1:T(8,128)}, u32[]{:S(2)}, u32[]{:S(2)}) async-start(f32[16,512,128]{2,0,1:T(8,128)} %copy.138), calls=%async_computation.6 | async-start | bytes 8388608 | tf_op jit(solution)/shard_map/all_to_all | solution.py:85
  723.1 53.4 %copy-start.12 = (f32[32,16,16,128]{3,1,0,2:T(8,128)}, f32[32,16,16,128]{3,1,0,2:T(8,128)S(1)}, u32[]{:S(2)}) copy-start(f32[32,16,16,128]{3,1,0,2:T(8,128)S(1)} %copy.145) | copy-start | bytes 12582916
  812.8 13.7 %copy-start.18 = (f32[512,16,128]{2,0,1:T(8,128)S(1)}, f32[512,16,128]{2,0,1:T(8,128)}, u32[]{:S(2)}) copy-start(f32[512,16,128]{2,0,1:T(8,128)} %fusion.31) | copy-start | bytes 12582916
  812.8 13.7 %copy-start.19 = (f32[512,16,128]{2,0,1:T(8,128)S(1)}, f32[512,16,128]{2,0,1:T(8,128)}, u32[]{:S(2)}) copy-start(f32[512,16,128]{2,0,1:T(8,128)} %fusion.14) | copy-start | bytes 12582916
  812.8 13.7 %copy-start.20 = (f32[512,16,128]{2,0,1:T(8,128)S(1)}, f32[512,16,128]{2,0,1:T(8,128)}, u32[]{:S(2)}) copy-start(f32[512,16,128]{2,0,1:T(8,128)} %fusion.29) | copy-start | bytes 12582916
  839.3 11.3 copy-start
  839.3 11.3 copy-start.13
  839.3 11.3 copy-start.16
  839.4 11.3 copy-start.17
  865.5 10.9 copy-start.2
  881.3 98.7 %all-to-all-start.9 = ((f32[512,16,128]{2,1,0:T(8,128)}), f32[512,16,128]{2,1,0:T(8,128)}, u32[]{:S(2)}, u32[]{:S(2)}) async-start(f32[512,16,128]{2,1,0:T(8,128)} %copy.149), calls=%async_computation.9 | async-start | bytes 8388608 | tf_op jit(solution)/shard_map/all_to_all | solution.py:114
  884.8 13.0 copy-start.1
  979.9 98.9 %all-to-all-start.8 = ((f32[512,16,128]{2,1,0:T(8,128)}), f32[512,16,128]{2,1,0:T(8,128)}, u32[]{:S(2)}, u32[]{:S(2)}) async-start(f32[512,16,128]{2,1,0:T(8,128)} %copy.146), calls=%async_computation.8 | async-start | bytes 8388608 | tf_op jit(solution)/shard_map/all_to_all | solution.py:113
  1078.8 4.8 copy-start.14
  1108.0 82.0 %all-to-all-start.11 = ((f32[16,512,128]{2,0,1:T(8,128)}), f32[16,512,128]{2,0,1:T(8,128)}, u32[]{:S(2)}, u32[]{:S(2)}) async-start(f32[16,512,128]{2,0,1:T(8,128)} %copy.157), calls=%async_computation.11 | async-start | bytes 8388608 | tf_op jit(solution)/shard_map/all_to_all | solution.py:120
  1112.7 19.6 %copy-start.8 = (f32[16,32,16,128]{3,2,1,0:T(8,128)S(1)}, f32[16,32,16,128]{3,2,1,0:T(8,128)}, u32[]{:S(2)}) copy-start(f32[16,32,16,128]{3,2,1,0:T(8,128)} %copy-done.7) | copy-start | bytes 12582916
  1190.0 139.1 %all-to-all-start.10 = ((f32[16,512,128]{2,0,1:T(8,128)}), f32[16,512,128]{2,0,1:T(8,128)}, u32[]{:S(2)}, u32[]{:S(2)}) async-start(f32[16,512,128]{2,0,1:T(8,128)} %copy.152), calls=%async_computation.10 | async-start | bytes 8388608 | tf_op jit(solution)/shard_map/all_to_all | solution.py:119
  1332.7 7.0 copy-start.15
  1332.7 7.0 copy-start.24
  (5 other events, 16.3 us)
where the time goes:
time: 1360 us; the launch traced here: 1350 us
  waiting for transfers between devices  558 us (41%)
  matrix products  441 us (32%)
  starting transfers between devices  130 us (10%)
  blocking collectives  113 us (8%)
  local copies, waits for them, and re-layouts  96.7 us (7%)
    psum x1, blocking collectives, local(): mass = lax.psum(jnp.sum(concentration), ('slab', 'pencil')) / (NX * NY * NZ)  113 us
    dot_general x6, matrix products, transform_axis(): jnp.einsum(form, cosines, real_part, precision=lax.Precision.HIGHEST)  96 us
    dot_general x6, matrix products, transform_axis(): jnp.einsum(form, sines, imag_part, precision=lax.Precision.HIGHEST)  94.9 us
    dot_general x6, matrix products, transform_axis(): jnp.einsum(form, sines, real_part, precision=lax.Precision.HIGHEST)  93.4 us
    dot_general x6, matrix products, transform_axis(): jnp.einsum(form, cosines, imag_part, precision=lax.Precision.HIGHEST)  92.5 us
    all_to_all x1, waiting for transfers between devices, local(): lax.all_to_all(back_real, ('slab', 'pencil'), split_axis=0, concat_axis=1...  72.2 us
    all_to_all x1, waiting for transfers between devices, local(): lax.all_to_all(cube_imag, 'pencil', split_axis=0, concat_axis=1, tiled=True)  67.1 us
    all_to_all x1, waiting for transfers between devices, local(): lax.all_to_all(back_imag, ('slab', 'pencil'), split_axis=0, concat_axis=1...  66.9 us
  transfers between devices with their start and end apart: 12, of which 11 were waited for; matrix products, arithmetic and copies ran while one was open for 30% of the time, Pallas kernels for 0%

commit v1 on v0

v1 whole, which is shorter than its diff:
```python
import functools
import math

import jax
import jax.numpy as jnp
import numpy as np
from jax import lax
from jax.experimental import pallas as pl
from jax.experimental.pallas import tpu as pltpu
from jax.sharding import PartitionSpec as P

time_step = 1.0
stiffness = 1.0
VMEM_LIMIT = 60 * 1024 * 1024
LANES = 128


def split_table(table):
    high = table.astype(np.float32).astype(jnp.bfloat16)
    low = (table - high.astype(np.float64)).astype(np.float32).astype(jnp.bfloat16)
    return jnp.asarray(np.stack([high, low]))


def angles(rows, columns, length):
    return 2.0 * np.pi / length * ((rows[:, None] * columns[None, :]) % length)


def half_tables(length):
    half = length // 2
    cell = np.arange(half)
    forward_left, forward_right, inverse_left, inverse_right = [], [], [], []
    for parity in range(2):
        angle = angles(2 * cell + parity, cell, length)
        cos, sin = np.cos(angle), np.sin(angle)
        forward_left.append(np.block([[cos, sin], [-sin, cos]]))
        forward_right.append(np.block([[cos.T, -sin.T], [sin.T, cos.T]]))
        inverse_left.append(np.block([[cos.T, -sin.T], [sin.T, cos.T]]))
        inverse_right.append(np.block([[cos, sin], [-sin, cos]]))
    return tuple(
        split_table(np.stack(t)) for t in (forward_left, forward_right, inverse_left, inverse_right)
    )


def split(value):
    high = value.astype(jnp.bfloat16)
    low = (value - high.astype(jnp.float32)).astype(jnp.bfloat16)
    return high, low


def dot3(left, right, dims=((1,), (0,))):
    dot = functools.partial(
        lax.dot_general, dimension_numbers=(dims, ((), ())), preferred_element_type=jnp.float32
    )
    return dot(left[0], right[0]) + (dot(left[0], right[1]) + dot(left[1], right[0]))


def depth_forward(field, table, chunks, devices):
    first, second, depth = field.shape
    per_chunk = table.shape[1] // chunks
    pieces = depth // LANES

    def kernel(*refs):
        field_refs, table_ref, out_refs = refs[:pieces], refs[pieces], refs[pieces + 1 :]
        weights = (table_ref[0], table_ref[1])

        def body(row, _):
            conc = jnp.concatenate(
                [ref.reshape(LANES * 8, LANES)[pl.ds(row, LANES, stride=8), :] for ref in field_refs],
                axis=1,
            )
            for which, value in enumerate((conc, conc * conc * conc)):
                result = dot3(weights, split(value), ((1,), (1,)))
                for chunk in range(chunks):
                    rows_out = out_refs[chunk].reshape(devices * 4 * 8, LANES)
                    for part in range(2):
                        start = chunk * per_chunk + part * devices
                        rows_out[pl.ds((2 * which + part) * 8 + row, devices, stride=32), :] = result[
                            start : start + devices
                        ]
            return 0

        lax.fori_loop(0, 8, body, 0)

    return pl.pallas_call(
        kernel,
        grid=(second // 8, first // LANES),
        in_specs=[
            pl.BlockSpec((LANES, 8, LANES), lambda i, j, k=k: (j, i, k)) for k in range(pieces)
        ]
        + [pl.BlockSpec(table.shape, lambda i, j: (0, 0, 0))],
        out_specs=[pl.BlockSpec((devices, 4, 8, LANES), lambda i, j: (0, 0, i, j))] * chunks,
        out_shape=[jax.ShapeDtypeStruct((devices, 4, second, first), jnp.float32)] * chunks,
        compiler_params=pltpu.CompilerParams(vmem_limit_bytes=VMEM_LIMIT),
        cost_estimate=pl.CostEstimate(
            flops=12 * first * second * depth * table.shape[1],
            bytes_accessed=12 * first * second * depth,
            transcendentals=0,
        ),
        name="depth_forward",
    )(*[field] * pieces, table)


def depth_inverse(parts, table):
    devices, _, second, first = parts[0].shape
    depth = table.shape[2]

    def kernel(*refs):
        part_refs, table_ref, out_ref = refs[:-2], refs[-2], refs[-1]
        rows_out = out_ref.reshape(LANES * 8, LANES)
        weights = (table_ref[0], table_ref[1])

        def body(row, _):
            lines = jnp.concatenate(
                [
                    ref.reshape(devices * 2 * 8, LANES)[pl.ds(row, devices * 2, stride=8), :]
                    for ref in part_refs
                ],
                axis=0,
            )
            rows_out[pl.ds(row, LANES, stride=8), :] = dot3(split(lines), weights, ((0,), (0,)))
            return 0

        lax.fori_loop(0, 8, body, 0)

    return pl.pallas_call(
        kernel,
        grid=(second // 8, first // LANES, depth // LANES),
        in_specs=[pl.BlockSpec((devices, 2, 8, LANES), lambda i, j, k: (0, 0, i, j))] * len(parts)
        + [pl.BlockSpec((2, table.shape[1], LANES), lambda i, j, k: (0, 0, k))],
        out_specs=pl.BlockSpec((LANES, 8, LANES), lambda i, j, k: (j, i, k)),
        out_shape=jax.ShapeDtypeStruct((first, second, depth), jnp.float32),
        compiler_params=pltpu.CompilerParams(vmem_limit_bytes=VMEM_LIMIT),
        cost_estimate=pl.CostEstimate(
            flops=6 * first * second * depth * table.shape[1],
            bytes_accessed=8 * first * second * depth,
            transcendentals=0,
        ),
        name="depth_inverse",
    )(*parts, table)


def plane_step(lines, depth_index, waves, tables_first, tables_second, scale):
    slabs, pencils, _, second, first = lines.shape
    rows, columns = pencils * second // 2, first
    wave_first, wave_second, wave_third = waves

    def kernel(index_ref, third_ref, lines_ref, wf_ref, ws_ref, fr_ref, fl_ref, il_ref, ir_ref, out_ref, mid_ref, back_ref):
        def whole(slab, part):
            return lines_ref[slab, :, part].reshape(2 * rows, columns)

        for which in range(2):
            for parity in range(2):
                joined = []
                for part in range(2):
                    one, two = whole(0, 2 * which + part), whole(1, 2 * which + part)
                    joined.append(one + two if parity == 0 else one - two)
                result = dot3(
                    split(jnp.concatenate(joined, axis=1)), (fr_ref[0, parity], fr_ref[1, parity])
                )
                mid_ref[which, parity] = result
        third = third_ref[index_ref[0]]
        for parity in range(2):
            for parity_second in range(2):
                spectra = []
                for which in range(2):
                    top = mid_ref[which, parity, :rows]
                    bottom = mid_ref[which, parity, rows:]
                    both = top + bottom if parity_second == 0 else top - bottom
                    stacked = jnp.concatenate([both[:, :columns], both[:, columns:]], axis=0)
                    spectra.append(
                        dot3((fl_ref[0, parity_second], fl_ref[1, parity_second]), split(stacked))
                    )
                wave_square = wf_ref[parity][None, :] + ws_ref[parity_second] + third
                divisor = 1.0 + time_step * stiffness * wave_square * wave_square
                retain = scale * (1.0 + time_step * wave_square) / divisor
                forcing = scale * (time_step * wave_square) / divisor
                fresh = jnp.concatenate(
                    [
                        retain * spectra[0][:rows] - forcing * spectra[1][:rows],
                        retain * spectra[0][rows:] - forcing * spectra[1][rows:],
                    ],
                    axis=0,
                )
                result = dot3((il_ref[0, parity_second], il_ref[1, parity_second]), split(fresh))
                back_ref[parity_second] = jnp.concatenate([result[:rows], result[rows:]], axis=1)
            mid_ref[0, parity, :rows] = back_ref[0] + back_ref[1]
            mid_ref[0, parity, rows:] = back_ref[0] - back_ref[1]
        for parity in range(2):
            mid_ref[1, parity] = dot3(split(mid_ref[0, parity]), (ir_ref[0, parity], ir_ref[1, parity]))
        for part in range(2):
            span = slice(part * columns, (part + 1) * columns)
            even, odd = mid_ref[1, 0, :, span], mid_ref[1, 1, :, span]
            out_ref[0, :, part] = (even + odd).reshape(pencils, second, first)
            out_ref[1, :, part] = (even - odd).reshape(pencils, second, first)

    vmem = pl.BlockSpec(memory_space=pltpu.VMEM)
    smem = pl.BlockSpec(memory_space=pltpu.SMEM)
    forward_left, _, inverse_left, _ = tables_second
    _, forward_right, _, inverse_right = tables_first
    work = 2 * rows * columns * (2 * columns + 2 * rows) * 12 * 6
    return pl.pallas_call(
        kernel,
        in_specs=[smem, smem] + [vmem] * 7,
        out_specs=vmem,
        out_shape=jax.ShapeDtypeStruct((slabs, pencils, 2, second, first), jnp.float32),
        scratch_shapes=[
            pltpu.VMEM((2, 2, 2 * rows, 2 * columns), jnp.float32),
            pltpu.VMEM((2, rows, 2 * columns), jnp.float32),
        ],
        compiler_params=pltpu.CompilerParams(vmem_limit_bytes=VMEM_LIMIT),
        cost_estimate=pl.CostEstimate(
            flops=work, bytes_accessed=6 * lines.size, transcendentals=0
        ),
        name="plane_step",
    )(depth_index, wave_third, lines, wave_first, wave_second, forward_right, forward_left, inverse_left, inverse_right)


def wave_squares(length):
    index = np.arange(length)
    signed = np.where(index < length // 2, index, index - length).astype(np.float32)
    return np.square(np.float32(2.0 * math.pi / length) * signed)


def local(concentration, slabs, pencils):
    devices = slabs * pencils
    first, second, depth = concentration.shape
    total_first, total_second = first * slabs, second * pencils
    kept = depth // 2
    chunks = kept // devices
    tables_first, tables_second = half_tables(total_first), half_tables(total_second)

    index = np.arange(kept).reshape(chunks, devices)
    angle = angles(index.reshape(-1), np.arange(depth), depth).reshape(chunks, devices, depth)
    forward = np.stack([np.cos(angle), -np.sin(angle)], axis=1).reshape(2 * kept, depth)
    weights = np.where(index == 0, 1.0, 2.0)[:, :, None]
    inverse = np.stack([weights * np.cos(angle), -weights * np.sin(angle)], axis=2)
    inverse = inverse.reshape(2 * kept, depth)

    parity_waves_first = jnp.asarray(wave_squares(total_first).reshape(-1, 2).T)
    parity_waves_second = jnp.asarray(wave_squares(total_second).reshape(-1, 2).T[:, :, None])
    third = jnp.asarray(wave_squares(depth)[:kept])
    waves = (parity_waves_first, parity_waves_second, third)
    me = lax.axis_index(("slab", "pencil"))
    scale = 1.0 / (total_first * total_second * depth)

    sent = depth_forward(concentration, split_table(forward), chunks, devices)
    back = []
    for chunk in range(chunks):
        lines = lax.all_to_all(sent[chunk], ("slab", "pencil"), split_axis=0, concat_axis=0, tiled=True)
        lines = lines.reshape(slabs, pencils, 4, second, first)
        fresh = plane_step(
            lines, (chunk * devices + me).reshape(1), waves, tables_first, tables_second, scale
        ).reshape(devices, 2, second, first)
        back.append(lax.all_to_all(fresh, ("slab", "pencil"), split_axis=0, concat_axis=0, tiled=True))
    updated = depth_inverse(back, split_table(inverse))
    mass = lax.psum(jnp.sum(concentration), ("slab", "pencil")) * scale
    return updated, mass


def solution(mesh):
    sizes = dict(mesh.shape)
    return jax.shard_map(
        functools.partial(local, slabs=sizes["slab"], pencils=sizes["pencil"]),
        mesh=mesh,
        in_specs=(P("slab", "pencil", None),),
        out_specs=(P("slab", "pencil", None), P()),
        check_vma=False,
    )
```

time: 1360 us -> 711 us (0.52)
  matrix products: 441 us -> 0 us
  waiting for transfers between devices: 558 us -> 171 us
  blocking collectives: 113 us -> 359 us
  Pallas kernels: 0 us -> 147 us
  starting transfers between devices: 130 us -> 16.8 us
  local copies, waits for them, and re-layouts: 96.7 us -> 0.01 us
    dot_general x30 -> x0, matrix products: 441 us -> none  [the longest x6 96 us: transform_axis(): jnp.einsum(form, cosines, real_part, precision=lax.Precision.HIGHEST)]
    all_to_all x12 -> x5, waiting for transfers between devices: 558 us -> 171 us  [the longest x4 94.3 us: local(): lax.all_to_all(fresh, ('slab', 'pencil'), split_axis=0, concat_axis=0, ti...]
    all_to_all x0 -> x3, blocking collectives: none -> 296 us  [local(): lax.all_to_all(sent[chunk], ('slab', 'pencil'), split_axis=0, concat_axis...]
    pallas_call x0 -> x6, Pallas kernels: none -> 147 us  [the longest x4 72.9 us: plane_step(): pl.pallas_call(kernel, in_specs=[smem, smem] + [vmem] * 7, out_specs=vmem...]
    all_to_all x12 -> x5, starting transfers between devices: 130 us -> 16.8 us  [the longest x4 13.2 us: local(): lax.all_to_all(fresh, ('slab', 'pencil'), split_axis=0, concat_axis=0, ti...]
    psum x1, blocking collectives: 113 us -> 62.7 us  [local(): mass = lax.psum(jnp.sum(concentration), ('slab', 'pencil')) * scale]
    all_to_all x12 -> x0, local copies, waits for them, and re-layouts: 39.3 us -> none  [the longest x1 5.51 us: local(): lax.all_to_all(columns[1], 'pencil', split_axis=1, concat_axis=0, tiled=T...]
    add x4 -> x0, local copies, waits for them, and re-layouts: 21.3 us -> none  [the longest x2 10.9 us: transform_axis(): return (cos_real + sin_imag, cos_imag - sin_real)]
  transfers between devices with their start and end apart: 12 -> 5, of which waited for: 11 -> 4; matrix products, arithmetic and copies ran while one was open for 30% -> 1% of each run, Pallas kernels for 0% -> 10%
where the time goes in v1:
time: 711 us; the launch traced here: 704 us
  blocking collectives  359 us (50%)
  waiting for transfers between devices  171 us (24%)
  Pallas kernels  147 us (21%)
  starting transfers between devices  16.8 us (2%)
    all_to_all x3, blocking collectives, local(): lax.all_to_all(sent[chunk], ('slab', 'pencil'), split_axis=0, concat_axis...  296 us
    all_to_all x4, waiting for transfers between devices, local(): lax.all_to_all(fresh, ('slab', 'pencil'), split_axis=0, concat_axis=0, ti...  94.3 us
    all_to_all x1, waiting for transfers between devices, local(): lax.all_to_all(sent[chunk], ('slab', 'pencil'), split_axis=0, concat_axis...  76.9 us
    pallas_call x4, Pallas kernels, plane_step(): pl.pallas_call(kernel, in_specs=[smem, smem] + [vmem] * 7, out_specs=vmem...  72.9 us
    psum x1, blocking collectives, local(): mass = lax.psum(jnp.sum(concentration), ('slab', 'pencil')) * scale  62.7 us
    pallas_call x1, Pallas kernels, depth_inverse(): pl.pallas_call(kernel, grid=(second // 8, first // LANES, depth // LANES)...  38.6 us
    pallas_call x1, Pallas kernels, depth_forward(): pl.pallas_call(kernel, grid=(second // 8, first // LANES), in_specs=[pl.B...  35.9 us
  transfers between devices with their start and end apart: 5, of which 4 were waited for; matrix products, arithmetic and copies ran while one was open for 1% of the time, Pallas kernels for 10%

profile of v1, /device:TPU:0, one launch (start us, length us, event | category | flops | bytes accessed | tf_op | source)
XLA Modules:
  0.0 703.6 jit_solution(10609801618276991299)
XLA Ops:
  0.6 35.9 %depth_forward.1 = (f32[32,4,32,256]{3,2,1,0:T(8,128)}, f32[32,4,32,256]{3,2,1,0:T(8,128)}, f32[32,4,32,256]{3,2,1,0:T(8,128)}, f32[32,4,32,256]{3,2,1,0:T(8,128)}) custom-call(f32[256,32,256]{2,1,0:T(8,128)} %refs_1_.1, f32[256,32,256]{2,1,0:T(8,128)} %refs_1_.1, bf16[2,256,256]{2,1,0:T(8,128)(2,1)} %constant.40.clone.refs_2_), custom_call_target="tpu_custom_call" | custom-call | flops 6442450944 | bytes 25165824 | tf_op jit(solution)/shard_map/depth_forward/pallas_call | solution.py:84
  36.5 0.0 copy-start.3
  36.5 102.1 %all_to_all.40 = f32[32,4,32,256]{3,2,1,0:T(8,128)} all-to-all(f32[32,4,32,256]{3,2,1,0:T(8,128)} %get-tuple-element.6), channel_id=1, replica_groups=mesh['slab'=2,'pencil'=16] {'slab','pencil'}, dimensions={0} | all-to-all | bytes 8388608 | tf_op jit(solution)/shard_map/all_to_all | solution.py:249
  138.6 0.0 copy-done.3
  138.6 0.0 copy-start.2
  138.6 97.2 %all_to_all.41 = f32[32,4,32,256]{3,2,1,0:T(8,128)} all-to-all(f32[32,4,32,256]{3,2,1,0:T(8,128)S(1)} %copy-done.3), channel_id=1, replica_groups=mesh['slab'=2,'pencil'=16] {'slab','pencil'}, dimensions={0} | all-to-all | bytes 8388608 | tf_op jit(solution)/shard_map/all_to_all | solution.py:249
  235.9 0.0 copy-done.2
  235.9 97.1 %all_to_all.42 = f32[32,4,32,256]{3,2,1,0:T(8,128)} all-to-all(f32[32,4,32,256]{3,2,1,0:T(8,128)S(1)} %copy-done.2), channel_id=1, replica_groups=mesh['slab'=2,'pencil'=16] {'slab','pencil'}, dimensions={0} | all-to-all | bytes 8388608 | tf_op jit(solution)/shard_map/all_to_all | solution.py:249
  332.9 3.6 all-to-all-start.6
  336.5 18.2 %plane_step.4 = f32[2,16,2,32,256]{4,3,2,1,0:T(8,128)} custom-call(s32[1]{0:T(128)} %bitcast.index_ref, f32[128]{0:T(128)} %constant.39.clone.third_ref, f32[2,16,4,32,256]{4,3,2,1,0:T(8,128)} %bitcast.14, f32[2,256]{1,0:T(2,128)} %constant.37.clone.wf_ref, f32[2,256,1]{2,1,0:T(8,128)} %constant.38.clone.ws_ref, ...), custom_call_target="tpu_custom_call" | custom-call | flops 9663676416 | bytes 6291456 | tf_op jit(solution)/shard_map/plane_step/pallas_call | solution.py:201
  354.7 76.9 %all-to-all-done.6 = f32[32,4,32,256]{3,2,1,0:T(8,128)} async-done(((f32[32,4,32,256]{3,2,1,0:T(8,128)}), f32[32,4,32,256]{3,2,1,0:T(8,128)}, u32[]{:S(2)}, u32[]{:S(2)}) %all-to-all-start.6) | async-done | bytes 4194336 | tf_op jit(solution)/shard_map/all_to_all | solution.py:249
  431.6 2.9 all-to-all-start.1
  434.5 18.2 %plane_step.5 = f32[2,16,2,32,256]{4,3,2,1,0:T(8,128)} custom-call(s32[1]{0:T(128)} %bitcast.3.index_ref, f32[128]{0:T(128)} %constant.39.clone.third_ref, f32[2,16,4,32,256]{4,3,2,1,0:T(8,128)} %bitcast.13, f32[2,256]{1,0:T(2,128)} %constant.37.clone.wf_ref, f32[2,256,1]{2,1,0:T(8,128)} %constant.38.clone.ws_ref, ...), custom_call_target="tpu_custom_call" | custom-call | flops 9663676416 | bytes 6291456 | tf_op jit(solution)/shard_map/plane_step/pallas_call | solution.py:201
  452.7 31.5 %all-to-all-done.1.refs_0_ = f32[32,2,32,256]{3,2,1,0:T(8,128)S(1)} async-done(((f32[32,2,32,256]{3,2,1,0:T(8,128)}), f32[32,2,32,256]{3,2,1,0:T(8,128)S(1)}, u32[]{:S(2)}, u32[]{:S(2)}) %all-to-all-start.1) | async-done | bytes 2097184 | tf_op jit(solution)/shard_map/all_to_all | solution.py:254
  484.2 0.0 copy-start
  484.2 3.8 all-to-all-start.3
  488.0 18.3 %plane_step.6 = f32[2,16,2,32,256]{4,3,2,1,0:T(8,128)} custom-call(s32[1]{0:T(128)} %bitcast.6.index_ref, f32[128]{0:T(128)} %constant.39.clone.third_ref, f32[2,16,4,32,256]{4,3,2,1,0:T(8,128)} %bitcast.12, f32[2,256]{1,0:T(2,128)} %constant.37.clone.wf_ref, f32[2,256,1]{2,1,0:T(8,128)} %constant.38.clone.ws_ref, ...), custom_call_target="tpu_custom_call" | custom-call | flops 9663676416 | bytes 6291456 | tf_op jit(solution)/shard_map/plane_step/pallas_call | solution.py:201
  506.3 0.0 copy-done
  506.3 31.3 %all-to-all-done.3.refs_1_ = f32[32,2,32,256]{3,2,1,0:T(8,128)} async-done(((f32[32,2,32,256]{3,2,1,0:T(8,128)}), f32[32,2,32,256]{3,2,1,0:T(8,128)}, u32[]{:S(2)}, u32[]{:S(2)}) %all-to-all-start.3) | async-done | bytes 2097184 | tf_op jit(solution)/shard_map/all_to_all | solution.py:254
  537.6 3.0 all-to-all-start.5
  540.6 18.2 %plane_step.7 = f32[2,16,2,32,256]{4,3,2,1,0:T(8,128)} custom-call(s32[1]{0:T(128)} %bitcast.9.index_ref, f32[128]{0:T(128)} %constant.39.clone.third_ref, f32[2,16,4,32,256]{4,3,2,1,0:T(8,128)} %bitcast.10.lines_ref, f32[2,256]{1,0:T(2,128)} %constant.37.clone.wf_ref, f32[2,256,1]{2,1,0:T(8,128)} %constant.38.clone.ws_ref, ...), custom_call_target="tpu_custom_call" | custom-call | flops 9663676416 | bytes 6291456 | tf_op jit(solution)/shard_map/plane_step/pallas_call | solution.py:201
  558.8 31.5 %all-to-all-done.5.refs_2_ = f32[32,2,32,256]{3,2,1,0:T(8,128)S(1)} async-done(((f32[32,2,32,256]{3,2,1,0:T(8,128)}), f32[32,2,32,256]{3,2,1,0:T(8,128)S(1)}, u32[]{:S(2)}, u32[]{:S(2)}) %all-to-all-start.5) | async-done | bytes 2097184 | tf_op jit(solution)/shard_map/all_to_all | solution.py:254
  590.3 0.0 copy-start.1
  590.3 3.6 all-to-all-start.7
  593.9 6.1 reduce_sum.9
  600.0 0.0 copy-done.1
  600.0 62.7 %psum.7 = f32[]{:T(128)} all-reduce(f32[]{:T(128)} %reduce_sum.9), channel_id=1, replica_groups=mesh['slab'=2,'pencil'=16] {'slab','pencil'}, use_global_device_ids=true, to_apply=%region_1.0 | all-reduce | flops 1 | bytes 8 | tf_op jit(solution)/shard_map/psum | solution.py:256
  663.4 0.0 all-to-all-done.7.refs_3_
  663.4 38.6 %depth_inverse.1 = f32[256,32,256]{2,1,0:T(8,128)} custom-call(f32[32,2,32,256]{3,2,1,0:T(8,128)} %copy-done, f32[32,2,32,256]{3,2,1,0:T(8,128)} %all-to-all-done.3.refs_1_, f32[32,2,32,256]{3,2,1,0:T(8,128)} %copy-done.1, f32[32,2,32,256]{3,2,1,0:T(8,128)} %all-to-all-done.7.refs_3_, bf16[2,256,256]{2,1,0:T(8,128)(2,1)} %constant.41.clone.refs_4_), custom_call_target="tpu_custom_call" | custom-call | flops 3221225472 | bytes 16777216 | tf_op jit(solution)/shard_map/depth_inverse/pallas_call | solution.py:125
Async XLA Ops:
  36.5 102.1 %copy-start.3 = (f32[32,4,32,256]{3,2,1,0:T(8,128)S(1)}, f32[32,4,32,256]{3,2,1,0:T(8,128)}, u32[]{:S(2)}) copy-start(f32[32,4,32,256]{3,2,1,0:T(8,128)} %get-tuple-element.7) | copy-start | bytes 12582916
  138.6 97.2 %copy-start.2 = (f32[32,4,32,256]{3,2,1,0:T(8,128)S(1)}, f32[32,4,32,256]{3,2,1,0:T(8,128)}, u32[]{:S(2)}) copy-start(f32[32,4,32,256]{3,2,1,0:T(8,128)} %get-tuple-element.8) | copy-start | bytes 12582916
  332.9 98.7 %all-to-all-start.6 = ((f32[32,4,32,256]{3,2,1,0:T(8,128)}), f32[32,4,32,256]{3,2,1,0:T(8,128)}, u32[]{:S(2)}, u32[]{:S(2)}) async-start(f32[32,4,32,256]{3,2,1,0:T(8,128)} %get-tuple-element.9), calls=%async_computation.6 | async-start | bytes 8388608 | tf_op jit(solution)/shard_map/all_to_all | solution.py:249
  431.6 52.6 %all-to-all-start.1 = ((f32[32,2,32,256]{3,2,1,0:T(8,128)}), f32[32,2,32,256]{3,2,1,0:T(8,128)S(1)}, u32[]{:S(2)}, u32[]{:S(2)}) async-start(f32[32,2,32,256]{3,2,1,0:T(8,128)} %bitcast.18), calls=%async_computation.1 | async-start | bytes 4194304 | tf_op jit(solution)/shard_map/all_to_all | solution.py:254
  484.2 22.1 %copy-start = (f32[32,2,32,256]{3,2,1,0:T(8,128)}, f32[32,2,32,256]{3,2,1,0:T(8,128)S(1)}, u32[]{:S(2)}) copy-start(f32[32,2,32,256]{3,2,1,0:T(8,128)S(1)} %all-to-all-done.1.refs_0_) | copy-start | bytes 6291460
  484.2 53.4 %all-to-all-start.3 = ((f32[32,2,32,256]{3,2,1,0:T(8,128)}), f32[32,2,32,256]{3,2,1,0:T(8,128)}, u32[]{:S(2)}, u32[]{:S(2)}) async-start(f32[32,2,32,256]{3,2,1,0:T(8,128)} %bitcast.17), calls=%async_computation.3 | async-start | bytes 4194304 | tf_op jit(solution)/shard_map/all_to_all | solution.py:254
  537.6 52.7 %all-to-all-start.5 = ((f32[32,2,32,256]{3,2,1,0:T(8,128)}), f32[32,2,32,256]{3,2,1,0:T(8,128)S(1)}, u32[]{:S(2)}, u32[]{:S(2)}) async-start(f32[32,2,32,256]{3,2,1,0:T(8,128)} %bitcast.16), calls=%async_computation.5 | async-start | bytes 4194304 | tf_op jit(solution)/shard_map/all_to_all | solution.py:254
  590.3 9.7 %copy-start.1 = (f32[32,2,32,256]{3,2,1,0:T(8,128)}, f32[32,2,32,256]{3,2,1,0:T(8,128)S(1)}, u32[]{:S(2)}) copy-start(f32[32,2,32,256]{3,2,1,0:T(8,128)S(1)} %all-to-all-done.5.refs_2_) | copy-start | bytes 6291460
  590.3 73.1 %all-to-all-start.7 = ((f32[32,2,32,256]{3,2,1,0:T(8,128)}), f32[32,2,32,256]{3,2,1,0:T(8,128)}, u32[]{:S(2)}, u32[]{:S(2)}) async-start(f32[32,2,32,256]{3,2,1,0:T(8,128)} %bitcast.15), calls=%async_computation.7 | async-start | bytes 4194304 | tf_op jit(solution)/shard_map/all_to_all | solution.py:254

commit v2 on v1

v2 whole, which is shorter than its diff:
```python
import functools
import math

import jax
import jax.numpy as jnp
import numpy as np
from jax import lax
from jax.experimental import pallas as pl
from jax.experimental.pallas import tpu as pltpu
from jax.sharding import Mesh
from jax.sharding import PartitionSpec as P


time_step = 1.0
stiffness = 1.0
VMEM_LIMIT = 60 * 1024 * 1024
LANES = 128
CHUNKS = [2, 2, 2, 2]


def split_table(table):
    high = table.astype(np.float32).astype(jnp.bfloat16)
    low = (table - high.astype(np.float64)).astype(np.float32).astype(jnp.bfloat16)
    return jnp.asarray(np.stack([high, low]))


def angles(rows, columns, length):
    return 2.0 * np.pi / length * ((rows[:, None] * columns[None, :]) % length)


def half_tables(length):
    half = length // 2
    cell = np.arange(half)
    forward_left, forward_right, inverse_left, inverse_right = [], [], [], []
    for parity in range(2):
        angle = angles(2 * cell + parity, cell, length)
        cos, sin = np.cos(angle), np.sin(angle)
        forward_left.append(np.block([[cos, sin], [-sin, cos]]))
        forward_right.append(np.block([[cos.T, -sin.T], [sin.T, cos.T]]))
        inverse_left.append(np.block([[cos.T, -sin.T], [sin.T, cos.T]]))
        inverse_right.append(np.block([[cos, sin], [-sin, cos]]))
    return tuple(
        split_table(np.stack(t)) for t in (forward_left, forward_right, inverse_left, inverse_right)
    )


def split(value):
    high = value.astype(jnp.bfloat16)
    low = (value - high.astype(jnp.float32)).astype(jnp.bfloat16)
    return high, low


def dot3(left, right, dims=((1,), (0,))):
    dot = functools.partial(
        lax.dot_general, dimension_numbers=(dims, ((), ())), preferred_element_type=jnp.float32
    )
    return dot(left[0], right[0]) + (dot(left[0], right[1]) + dot(left[1], right[0]))


def depth_forward(field, table, counts, devices):
    first, second, depth = field.shape
    pieces = depth // LANES
    shapes = [(devices, count, 4, second, first) for count in counts]

    def kernel(*refs):
        field_refs, table_ref, out_refs = refs[:pieces], refs[pieces], refs[pieces + 1 :]
        weights = (table_ref[0], table_ref[1])

        def body(row, _):
            conc = jnp.concatenate(
                [
                    ref.reshape(LANES * 8, LANES)[pl.ds(row, LANES, stride=8), :].T
                    for ref in field_refs
                ],
                axis=0,
            )
            for which, value in enumerate((conc, conc * conc * conc)):
                result = dot3(weights, split(value))
                start = 0
                for count, out_ref in zip(counts, out_refs):
                    rows_out = out_ref.reshape(devices * count * 4 * 8, LANES)
                    for index in range(count):
                        for part in range(2):
                            place = (index * 4 + 2 * which + part) * 8 + row
                            rows_out[pl.ds(place, devices, stride=count * 32), :] = result[
                                start : start + devices
                            ]
                            start += devices
            return 0

        lax.fori_loop(0, 8, body, 0, unroll=8)

    return pl.pallas_call(
        kernel,
        grid=(second // 8, first // LANES),
        in_specs=[
            pl.BlockSpec((LANES, 8, LANES), lambda i, j, k=k: (j, i, k)) for k in range(pieces)
        ]
        + [pl.BlockSpec(table.shape, lambda i, j: (0, 0, 0))],
        out_specs=[pl.BlockSpec((*s[:3], 8, LANES), lambda i, j: (0, 0, 0, i, j)) for s in shapes],
        out_shape=[jax.ShapeDtypeStruct(s, jnp.float32) for s in shapes],
        compiler_params=pltpu.CompilerParams(vmem_limit_bytes=VMEM_LIMIT),
        cost_estimate=pl.CostEstimate(
            flops=12 * first * second * depth * table.shape[1],
            bytes_accessed=4 * first * second * (depth + 2 * table.shape[1]),
            transcendentals=0,
        ),
        name="depth_forward",
    )(*[field] * pieces, table)


def depth_inverse(parts, table, before=None):
    devices, _, _, second, first = parts[0].shape
    counts = [part.shape[1] for part in parts]
    depth = table.shape[2]
    last = before is not None
    width = LANES if last else depth

    def kernel(*refs):
        part_refs, table_ref, out_ref = refs[: len(parts)], refs[len(parts)], refs[-1]
        weights = (table_ref[0], table_ref[1])

        def body(row, _):
            lines = jnp.concatenate(
                [
                    ref.reshape(devices * count * 2 * 8, LANES)[
                        pl.ds(row, devices * count * 2, stride=8), :
                    ]
                    for ref, count in zip(part_refs, counts)
                ],
                axis=0,
            )
            result = dot3(split(lines.T), weights)
            if last:
                out_ref.reshape(LANES * 8, LANES)[pl.ds(row, LANES, stride=8), :] = result + refs[-2][row]
            else:
                out_ref[row] = result
            return 0

        lax.fori_loop(0, 8, body, 0, unroll=8)

    by_second = pl.BlockSpec((8, LANES, width), lambda i, j, k: (i, j, k))
    by_first = pl.BlockSpec((LANES, 8, width), lambda i, j, k: (j, i, k))
    out = (first, second, depth) if last else (second, first, depth)
    return pl.pallas_call(
        kernel,
        grid=(second // 8, first // LANES, depth // width),
        in_specs=[
            pl.BlockSpec((devices, count, 2, 8, LANES), lambda i, j, k: (0, 0, 0, i, j))
            for count in counts
        ]
        + [pl.BlockSpec((2, table.shape[1], width), lambda i, j, k: (0, 0, k))]
        + [by_second] * last,
        out_specs=by_first if last else by_second,
        out_shape=jax.ShapeDtypeStruct(out, jnp.float32),
        compiler_params=pltpu.CompilerParams(vmem_limit_bytes=VMEM_LIMIT),
        cost_estimate=pl.CostEstimate(
            flops=6 * first * second * depth * table.shape[1],
            bytes_accessed=4 * first * second * (depth * (1 + last) + table.shape[1]),
            transcendentals=0,
        ),
        name="depth_inverse",
    )(*parts, table, *([before] if last else []))


def plane_forward(lines, depth_index, waves, tables_first, tables_second, scale):
    slabs, others, count, _, second, first = lines.shape
    rows, columns = others * second, first
    wave_first, wave_second, wave_third = waves

    def kernel(index_ref, third_ref, lines_ref, wf_ref, ws_ref, fr_ref, fl_ref, il_ref, own_ref, other_ref, mid_ref):
        third_index = index_ref[0] + pl.program_id(0) * index_ref[1]
        carries = jnp.where(third_index == 0, 0.0, 1.0)
        for which in range(2):
            for parity in range(2):
                joined = []
                for part in range(2):
                    one, two = (
                        lines_ref[slab, :, 0, 2 * which + part].reshape(rows, columns) for slab in range(2)
                    )
                    value = one + two if parity == 0 else one - two
                    joined.append(value * carries if (which, part) == (0, 1) else value)
                result = dot3(
                    split(jnp.concatenate(joined, axis=1)), (fr_ref[0, parity], fr_ref[1, parity])
                )
                mid_ref[which, parity, :rows] = result[:, :columns]
                mid_ref[which, parity, rows:] = result[:, columns:]
        third = third_ref[third_index]
        for parity in range(2):
            stacked = [split(mid_ref[which, parity]) for which in range(2)]
            back = []
            for parity_second in range(2):
                table = (fl_ref[0, parity_second], fl_ref[1, parity_second])
                spectra = [dot3(table, stacked[which]) for which in range(2)]
                wave_square = wf_ref[parity][None, :] + ws_ref[parity_second] + third
                divisor = 1.0 + time_step * stiffness * wave_square * wave_square
                retain = scale * (1.0 + time_step * wave_square) / divisor
                forcing = scale * (time_step * wave_square) / divisor
                fresh = jnp.concatenate(
                    [
                        retain * spectra[0][:rows] - forcing * spectra[1][:rows],
                        retain * spectra[0][rows:] - forcing * spectra[1][rows:],
                    ],
                    axis=0,
                )
                back.append(dot3((il_ref[0, parity_second], il_ref[1, parity_second]), split(fresh)))
            for out_ref, value in ((own_ref, back[0] + back[1]), (other_ref, back[0] - back[1])):
                out_ref[0, parity, :, :columns] = value[:rows]
                out_ref[0, parity, :, columns:] = value[rows:]

    smem = pl.BlockSpec(memory_space=pltpu.SMEM)
    fixed = lambda a: pl.BlockSpec(a.shape, lambda i: (0,) * a.ndim)
    forward_left, _, inverse_left, _ = tables_second
    _, forward_right, _, _ = tables_first
    consts = (wave_first, wave_second, forward_right, forward_left, inverse_left)
    out = (count, 2, rows, 2 * columns)
    return pl.pallas_call(
        kernel,
        grid=(count,),
        in_specs=[smem, smem, pl.BlockSpec((slabs, others, 1, 4, second, first), lambda i: (0, 0, i, 0, 0, 0))]
        + [fixed(a) for a in consts],
        out_specs=[pl.BlockSpec((1, *out[1:]), lambda i: (i, 0, 0, 0))] * 2,
        out_shape=[jax.ShapeDtypeStruct(out, jnp.float32)] * 2,
        scratch_shapes=[pltpu.VMEM((2, 2, 2 * rows, columns), jnp.float32)],
        compiler_params=pltpu.CompilerParams(vmem_limit_bytes=VMEM_LIMIT),
        cost_estimate=pl.CostEstimate(
            flops=count * 6 * 4 * rows * columns * (4 * columns + 12 * rows),
            bytes_accessed=8 * lines.size,
            transcendentals=0,
        ),
        name="plane_forward",
    )(depth_index, wave_third, lines, *consts)


def plane_inverse(own, near, far, tables_first, second):
    count, _, rows, columns = own.shape
    columns //= 2
    others = rows // second

    def kernel(own_ref, near_ref, far_ref, ir_ref, out_ref):
        even, odd = (
            dot3(split(own_ref[0, p] + (near_ref[0, p] + far_ref[0, p])), (ir_ref[0, p], ir_ref[1, p]))
            for p in range(2)
        )
        for slab, value in enumerate((even + odd, even - odd)):
            for part in range(2):
                span = slice(part * columns, (part + 1) * columns)
                out_ref[slab, :, 0, part] = value[:, span].reshape(others, second, columns)

    table = tables_first[3]
    spec = pl.BlockSpec((1, *own.shape[1:]), lambda i: (i, 0, 0, 0))
    return pl.pallas_call(
        kernel,
        grid=(count,),
        in_specs=[spec, spec, spec, pl.BlockSpec(table.shape, lambda i: (0, 0, 0, 0))],
        out_specs=pl.BlockSpec((2, others, 1, 2, second, columns), lambda i: (0, 0, i, 0, 0, 0)),
        out_shape=jax.ShapeDtypeStruct((2, others, count, 2, second, columns), jnp.float32),
        compiler_params=pltpu.CompilerParams(vmem_limit_bytes=VMEM_LIMIT),
        cost_estimate=pl.CostEstimate(
            flops=count * 6 * 4 * rows * columns * 2 * columns,
            bytes_accessed=12 * own.size,
            transcendentals=0,
        ),
        name="plane_inverse",
    )(own, near, far, table)


def wave_squares(length):
    index = np.arange(length)
    signed = np.where(index < length // 2, index, index - length).astype(np.float32)
    return np.square(np.float32(2.0 * math.pi / length) * signed)


def chunk_counts(total):
    return CHUNKS if sum(CHUNKS) == total else [1] * total


def local(concentration, slabs, others):
    devices = slabs * others
    first, second, depth = concentration.shape
    total_first, total_second = first * slabs, 2 * second * others
    kept = depth // 2
    counts = chunk_counts(kept // devices)
    zero_chunk = min(1, len(counts) - 1)
    starts = [0] * len(counts)
    for chunk in range(len(counts)):
        if chunk != zero_chunk:
            starts[chunk] = counts[zero_chunk] + sum(
                counts[c] for c in range(chunk) if c != zero_chunk
            )
    tables_first, tables_second = half_tables(total_first), half_tables(total_second)

    mirrored = np.arange(devices) ^ (others // 2)

    def by_half(rows, axis):
        return np.stack([r.reshape(-1, depth) for r in (rows, np.take(rows, mirrored, axis))])

    half = lax.axis_index("half")

    def table_of(pair):
        return lax.dynamic_index_in_dim(split_table(pair), half, 1, keepdims=False)

    forward, inverse = [], []
    for start, count in zip(starts, counts):
        index = np.arange(start * devices, (start + count) * devices)
        angle = angles(index, np.arange(depth), depth).reshape(count, devices, depth)
        forward.append(by_half(np.stack([np.cos(angle), -np.sin(angle)], axis=1), 2))
        weights = np.where(index == 0, 1.0, 2.0).reshape(count, devices, 1)
        waves = np.stack([weights * np.cos(angle), -weights * np.sin(angle)], axis=2)
        inverse.append(by_half(waves.transpose(1, 0, 2, 3), 0))

    parity_waves_first = jnp.asarray(wave_squares(total_first).reshape(-1, 2).T)
    parity_waves_second = jnp.asarray(wave_squares(total_second).reshape(-1, 2).T[:, :, None])
    third = jnp.asarray(wave_squares(depth)[:kept])
    waves = (parity_waves_first, parity_waves_second, third)
    group = ("slab", "other")
    me = lax.axis_index(group) ^ (half * (others // 2))
    scale = 1.0 / (total_first * total_second * depth)

    partners = [(i, others + (i ^ (others // 2))) for i in range(others)]
    both_ways = [((a, b), (b, a)) for a, b in partners]
    far_pairs = [pair for way in both_ways[: others // 2] for pair in way]
    near_pairs = [pair for way in both_ways[others // 2 :] for pair in way]

    def exchange(value):
        return lax.all_to_all(value, group, split_axis=0, concat_axis=0, tiled=True)

    sent = depth_forward(concentration, table_of(forward[0]), counts[:1], devices)
    sent += depth_forward(
        concentration, table_of(np.concatenate(forward[1:], axis=1)), counts[1:], devices
    )
    sent = list(sent)
    is_zero, zero_place = me == 0, half * (others // 2)
    mass = jnp.sum(concentration)
    sent[zero_chunk] = sent[zero_chunk].at[zero_place, 0, 1, 0, 0].set(mass)
    back = []
    for chunk, count in enumerate(counts):
        lines = exchange(sent[chunk])
        lines = lines.reshape(slabs, others, count, 4, second, first)
        if chunk == zero_chunk:
            mass = jnp.sum(lines[:, :, 0, 1, 0, 0])
        index = jnp.stack([starts[chunk] * devices + me, jnp.int32(devices)])
        own, other = plane_forward(lines, index, waves, tables_first, tables_second, scale)
        if chunk == zero_chunk:
            spot = (0, 0, 0, first)
            other = other.at[spot].set(jnp.where(is_zero, mass, other[spot]))
        near = lax.ppermute(other, ("half", "other"), near_pairs)
        far = lax.ppermute(other, ("half", "other"), far_pairs)
        if chunk == zero_chunk:
            mass += near[spot] + far[spot]
            near = near.at[spot].set(jnp.where(is_zero, 0.0, near[spot]))
            far = far.at[spot].set(jnp.where(is_zero, 0.0, far[spot]))
        fresh = plane_inverse(own, near, far, tables_first, second)
        if chunk == zero_chunk:
            spot = (slice(None), slice(None), 0, 1, 0, 0)
            fresh = fresh.at[spot].set(jnp.where(is_zero, mass, fresh[spot]))
        back.append(exchange(fresh.reshape(devices, count, 2, second, first)))
    updated = depth_inverse(back[:-1], table_of(np.concatenate(inverse[:-1], axis=1)))
    updated = depth_inverse(back[-1:], table_of(inverse[-1]), updated)
    mass = back[zero_chunk][zero_place, 0, 1, 0, 0] * scale
    return updated, mass


def solution(mesh):
    slabs, pencils = mesh.shape["slab"], mesh.shape["pencil"]
    halves = Mesh(mesh.devices.reshape(slabs, 2, pencils // 2), ("slab", "half", "other"))
    field = P("slab", ("half", "other"), None)

    def body(concentration):
        return local(concentration, slabs, pencils // 2)

    return jax.shard_map(
        body, mesh=halves, in_specs=(field,), out_specs=(field, P()), check_vma=False
    )
```

time: 711 us -> 779 us (1.096)
  blocking collectives: 359 us -> 54.4 us
  starting transfers between devices: 16.8 us -> 208 us
  waiting for transfers between devices: 171 us -> 305 us
  Pallas kernels: 147 us -> 173 us
  local copies, waits for them, and re-layouts: 0.01 us -> 15.6 us
  other arithmetic: 6.14 us -> 15 us
    all_to_all x3 -> x1, blocking collectives: 296 us -> 54.4 us  [exchange(): return lax.all_to_all(value, group, split_axis=0, concat_axis=0, tiled=True)]
    ppermute x0 -> x8, waiting for transfers between devices: none -> 208 us  [the longest x4 208 us: local(): far = lax.ppermute(other, ('half', 'other'), far_pairs)]
    all_to_all x5 -> x7, starting transfers between devices: 16.8 us -> 180 us  [exchange(): return lax.all_to_all(value, group, split_axis=0, concat_axis=0, tiled=True)]
    all_to_all x5 -> x7, waiting for transfers between devices: 171 us -> 97.6 us  [exchange(): return lax.all_to_all(value, group, split_axis=0, concat_axis=0, tiled=True)]
    psum x1 -> x0, blocking collectives: 62.7 us -> none  [local(): mass = lax.psum(jnp.sum(concentration), ('slab', 'pencil')) * scale]
    ppermute x0 -> x8, starting transfers between devices: none -> 28.7 us  [the longest x4 20.5 us: local(): far = lax.ppermute(other, ('half', 'other'), far_pairs)]
    pallas_call x5 -> x10, Pallas kernels: 111 us -> 140 us  [the longest x4 90.3 us: plane_forward(): pl.pallas_call(kernel, grid=(count,), in_specs=[smem, smem, pl.BlockSpec(...]
    pallas_call x1 -> x2, Pallas kernels: 35.9 us -> 33 us  [depth_forward(): pl.pallas_call(kernel, grid=(second // 8, first // LANES), in_specs=[pl.B...]
  transfers between devices with their start and end apart: 5 -> 15, of which waited for: 4 -> 7; matrix products, arithmetic and copies ran while one was open for 1% -> 3% of each run, Pallas kernels for 10% -> 19%
where the time goes in v2:
time: 779 us; the launch traced here: 777 us
  waiting for transfers between devices  305 us (39%)
  starting transfers between devices  208 us (27%)
  Pallas kernels  173 us (22%)
  blocking collectives  54.4 us (7%)
  local copies, waits for them, and re-layouts  15.6 us (2%)
  other arithmetic  15 us (2%)
    ppermute x4, waiting for transfers between devices, local(): far = lax.ppermute(other, ('half', 'other'), far_pairs)  208 us
    all_to_all x7, starting transfers between devices, exchange(): return lax.all_to_all(value, group, split_axis=0, concat_axis=0, tiled=True)  180 us
    all_to_all x7, waiting for transfers between devices, exchange(): return lax.all_to_all(value, group, split_axis=0, concat_axis=0, tiled=True)  97.6 us
    pallas_call x4, Pallas kernels, plane_forward(): pl.pallas_call(kernel, grid=(count,), in_specs=[smem, smem, pl.BlockSpec(...  90.3 us
    all_to_all x1, blocking collectives, exchange(): return lax.all_to_all(value, group, split_axis=0, concat_axis=0, tiled=True)  54.4 us
    pallas_call x2, Pallas kernels, depth_forward(): pl.pallas_call(kernel, grid=(second // 8, first // LANES), in_specs=[pl.B...  33 us
    pallas_call x2, Pallas kernels, depth_inverse(): pl.pallas_call(kernel, grid=(second // 8, first // LANES, depth // width)...  26 us
    pallas_call x4, Pallas kernels, plane_inverse(): pl.pallas_call(kernel, grid=(count,), in_specs=[spec, spec, spec, pl.Bloc...  23.8 us
  transfers between devices with their start and end apart: 15, of which 7 were waited for; matrix products, arithmetic and copies ran while one was open for 3% of the time, Pallas kernels for 19%

profile of v2, /device:TPU:0, one launch (start us, length us, event | category | flops | bytes accessed | tf_op | source)
XLA Modules:
  0.0 777.4 jit_solution(15906185061684798916)
XLA Ops:
  2.1 11.7 %depth_forward.3 = f32[16,2,4,32,256]{4,3,2,1,0:T(8,128)} custom-call(f32[256,32,256]{2,1,0:T(8,128)} %refs_1_.3, f32[256,32,256]{2,1,0:T(8,128)} %refs_1_.3, bf16[2,64,256]{2,1,0:T(8,128)(2,1)} %dynamic-slice_bitcast_fusion.2.refs_2_), custom_call_target="tpu_custom_call" | custom-call | flops 1610612736 | bytes 12582912 | tf_op jit(solution)/shard_map/depth_forward/pallas_call | solution.py:93
  13.8 6.5 all-to-all-start.2
  21.0 21.3 %depth_forward.2 = (f32[16,2,4,32,256]{4,3,2,1,0:T(8,128)}, f32[16,2,4,32,256]{4,3,2,1,0:T(8,128)}, f32[16,2,4,32,256]{4,3,2,1,0:T(8,128)}) custom-call(f32[256,32,256]{2,1,0:T(8,128)} %refs_1_.3, f32[256,32,256]{2,1,0:T(8,128)} %refs_1_.3, bf16[2,192,256]{2,1,0:T(8,128)(2,1)} %dynamic-slice_bitcast_fusion.1.refs_2_), custom_call_target="tpu_custom_call" | custom-call | flops 4831838208 | bytes 20971520 | tf_op jit(solution)/shard_map/depth_forward/pallas_call | solution.py:93
  42.3 35.2 %all-to-all-done.2 = f32[16,2,4,32,256]{4,3,2,1,0:T(8,128)} async-done(((f32[16,2,4,32,256]{4,3,2,1,0:T(8,128)}), f32[16,2,4,32,256]{4,3,2,1,0:T(8,128)}, u32[]{:S(2)}, u32[]{:S(2)}) %all-to-all-start.2) | async-done | bytes 4194336 | tf_op jit(solution)/shard_map/all_to_all | solution.py:326
  77.5 54.4 %all_to_all.40 = f32[16,2,4,32,256]{4,3,2,1,0:T(8,128)} all-to-all(f32[16,2,4,32,256]{4,3,2,1,0:T(8,128)} %get-tuple-element.73), channel_id=1, replica_groups=mesh['slab'=2,'half'=2,'other'=8] {'slab','other'}, dimensions={0} | all-to-all | bytes 8388608 | tf_op jit(solution)/shard_map/all_to_all | solution.py:326
  131.9 4.6 all-to-all-start.6
  136.5 6.2 reduce_sum.18
  148.0 45.5 %all-to-all-done.6 = f32[16,2,4,32,256]{4,3,2,1,0:T(8,128)} async-done(((f32[16,2,4,32,256]{4,3,2,1,0:T(8,128)}), f32[16,2,4,32,256]{4,3,2,1,0:T(8,128)}, u32[]{:S(2)}, u32[]{:S(2)}) %all-to-all-start.6) | async-done | bytes 4194336 | tf_op jit(solution)/shard_map/all_to_all | solution.py:326
  193.5 4.6 all-to-all-start.4
  198.7 22.5 %plane_forward.5 = (f32[2,2,256,512]{3,2,1,0:T(8,128)}, f32[2,2,256,512]{3,2,1,0:T(8,128)}) custom-call(s32[2]{0:T(128)} %pad_add_fusion.2.index_ref, f32[128]{0:T(128)} %constant.202.clone.third_ref, f32[2,8,2,4,32,256]{5,4,3,2,1,0:T(8,128)} %bitcast.7.lines_ref, f32[2,256]{1,0:T(2,128)} %constant.200.clone.wf_ref, f32[2,256,1]{2,1,0:T(8,128)} %constant.201.clone.ws_ref, ...), custom_call_target="tpu_custom_call" | custom-call | flops 12884901888 | bytes 8388608 | tf_op jit(solution)/shard_map/plane_forward/pallas_call | solution.py:217
  221.2 5.7 collective-permute-start.3
  228.9 72.8 %collective-permute-done.3.far_ref = f32[2,2,256,512]{3,2,1,0:T(8,128)S(1)} collective-permute-done((f32[2,2,256,512]{3,2,1,0:T(8,128)}, f32[2,2,256,512]{3,2,1,0:T(8,128)S(1)}, u32[]{:S(2)}, u32[]{:S(2)}) %collective-permute-start.3) | collective-permute-done | bytes 2097184 | tf_op jit(solution)/shard_map/ppermute | solution.py:348
  303.0 5.9 plane_inverse.5
  309.0 18.8 %all-to-all-start.3 = ((f32[16,2,2,32,256]{4,3,2,1,0:T(8,128)}), f32[16,2,2,32,256]{4,3,2,1,0:T(8,128)S(1)}, u32[]{:S(2)}, u32[]{:S(2)}) async-start(f32[16,2,2,32,256]{4,3,2,1,0:T(8,128)} %bitcast.32), calls=%async_computation.3 | async-start | bytes 4194304 | tf_op jit(solution)/shard_map/all_to_all | solution.py:326
  328.4 22.7 %plane_forward.7 = (f32[2,2,256,512]{3,2,1,0:T(8,128)}, f32[2,2,256,512]{3,2,1,0:T(8,128)}) custom-call(s32[2]{0:T(128)} %pad_add_fusion.index_ref, f32[128]{0:T(128)} %constant.202.clone.third_ref, f32[2,8,2,4,32,256]{5,4,3,2,1,0:T(8,128)} %bitcast.22.lines_ref, f32[2,256]{1,0:T(2,128)} %constant.200.clone.wf_ref, f32[2,256,1]{2,1,0:T(8,128)} %constant.201.clone.ws_ref, ...), custom_call_target="tpu_custom_call" | custom-call | flops 12884901888 | bytes 8388608 | tf_op jit(solution)/shard_map/plane_forward/pallas_call | solution.py:217
  351.1 4.9 collective-permute-start.7
  358.0 45.0 %collective-permute-done.7.far_ref = f32[2,2,256,512]{3,2,1,0:T(8,128)} collective-permute-done((f32[2,2,256,512]{3,2,1,0:T(8,128)}, f32[2,2,256,512]{3,2,1,0:T(8,128)}, u32[]{:S(2)}, u32[]{:S(2)}) %collective-permute-start.7) | collective-permute-done | bytes 2097184 | tf_op jit(solution)/shard_map/ppermute | solution.py:348
  403.1 6.0 plane_inverse.7
  410.4 48.8 %all-to-all-start.7 = ((f32[16,2,2,32,256]{4,3,2,1,0:T(8,128)}), f32[16,2,2,32,256]{4,3,2,1,0:T(8,128)}, u32[]{:S(2)}, u32[]{:S(2)}) async-start(f32[16,2,2,32,256]{4,3,2,1,0:T(8,128)} %bitcast.31), calls=%async_computation.7 | async-start | bytes 4194304 | tf_op jit(solution)/shard_map/all_to_all | solution.py:326
  459.9 22.6 %plane_forward.6 = (f32[2,2,256,512]{3,2,1,0:T(8,128)}, f32[2,2,256,512]{3,2,1,0:T(8,128)}) custom-call(s32[2]{0:T(128)} %pad_add_fusion.1.index_ref, f32[128]{0:T(128)} %constant.202.clone.third_ref, f32[2,8,2,4,32,256]{5,4,3,2,1,0:T(8,128)} %bitcast.13.lines_ref, f32[2,256]{1,0:T(2,128)} %constant.200.clone.wf_ref, f32[2,256,1]{2,1,0:T(8,128)} %constant.201.clone.ws_ref, ...), custom_call_target="tpu_custom_call" | custom-call | flops 12884901888 | bytes 8388608 | tf_op jit(solution)/shard_map/plane_forward/pallas_call | solution.py:217
  488.0 5.4 collective-permute-start.5
  495.4 44.5 %collective-permute-done.5 = f32[2,2,256,512]{3,2,1,0:T(8,128)S(1)} collective-permute-done((f32[2,2,256,512]{3,2,1,0:T(8,128)}, f32[2,2,256,512]{3,2,1,0:T(8,128)S(1)}, u32[]{:S(2)}, u32[]{:S(2)}) %collective-permute-start.5) | collective-permute-done | bytes 2097184 | tf_op jit(solution)/shard_map/ppermute | solution.py:348
  546.3 5.9 plane_inverse.6
  554.7 47.7 %all-to-all-start.5 = ((f32[16,2,2,32,256]{4,3,2,1,0:T(8,128)}), f32[16,2,2,32,256]{4,3,2,1,0:T(8,128)S(1)}, u32[]{:S(2)}, u32[]{:S(2)}) async-start(f32[16,2,2,32,256]{4,3,2,1,0:T(8,128)} %bitcast.30), calls=%async_computation.5 | async-start | bytes 4194304 | tf_op jit(solution)/shard_map/all_to_all | solution.py:326
  603.0 22.6 %plane_forward.4 = (f32[2,2,256,512]{3,2,1,0:T(8,128)}, f32[2,2,256,512]{3,2,1,0:T(8,128)}) custom-call(s32[2]{0:T(128)} %pad_add_fusion.3.index_ref, f32[128]{0:T(128)} %constant.202.clone.third_ref, f32[2,8,2,4,32,256]{5,4,3,2,1,0:T(8,128)} %bitcast.34, f32[2,256]{1,0:T(2,128)} %constant.200.clone.wf_ref, f32[2,256,1]{2,1,0:T(8,128)} %constant.201.clone.ws_ref, ...), custom_call_target="tpu_custom_call" | custom-call | flops 12884901888 | bytes 8388608 | tf_op jit(solution)/shard_map/plane_forward/pallas_call | solution.py:217
  625.6 4.6 collective-permute-start.1
  632.3 45.4 %collective-permute-done.1.far_ref = f32[2,2,256,512]{3,2,1,0:T(8,128)} collective-permute-done((f32[2,2,256,512]{3,2,1,0:T(8,128)}, f32[2,2,256,512]{3,2,1,0:T(8,128)}, u32[]{:S(2)}, u32[]{:S(2)}) %collective-permute-start.1) | collective-permute-done | bytes 2097184 | tf_op jit(solution)/shard_map/ppermute | solution.py:348
  677.6 5.9 plane_inverse.4
  683.6 49.0 %all-to-all-start.1 = ((f32[16,2,2,32,256]{4,3,2,1,0:T(8,128)}), f32[16,2,2,32,256]{4,3,2,1,0:T(8,128)}, u32[]{:S(2)}, u32[]{:S(2)}) async-start(f32[16,2,2,32,256]{4,3,2,1,0:T(8,128)} %bitcast.33), calls=%async_computation.1 | async-start | bytes 4194304 | tf_op jit(solution)/shard_map/all_to_all | solution.py:326
  734.4 10.3 %depth_inverse.2.refs_2_ = f32[32,256,256]{2,1,0:T(8,128)} custom-call(f32[16,2,2,32,256]{4,3,2,1,0:T(8,128)} %copy-done, f32[16,2,2,32,256]{4,3,2,1,0:T(8,128)} %copy-done.1, f32[16,2,2,32,256]{4,3,2,1,0:T(8,128)} %all-to-all-done.7.refs_2_, bf16[2,192,256]{2,1,0:T(8,128)(2,1)} %dynamic-slice_bitcast_fusion.refs_3_), custom_call_target="tpu_custom_call" | custom-call | flops 2415919104 | bytes 14680064 | tf_op jit(solution)/shard_map/depth_inverse/pallas_call | solution.py:145
  744.8 16.9 %all-to-all-done.1.refs_0_ = f32[16,2,2,32,256]{4,3,2,1,0:T(8,128)} async-done(((f32[16,2,2,32,256]{4,3,2,1,0:T(8,128)}), f32[16,2,2,32,256]{4,3,2,1,0:T(8,128)}, u32[]{:S(2)}, u32[]{:S(2)}) %all-to-all-start.1) | async-done | bytes 2097184 | tf_op jit(solution)/shard_map/all_to_all | solution.py:326
  761.7 15.7 %depth_inverse.3 = f32[256,32,256]{2,1,0:T(8,128)} custom-call(f32[16,2,2,32,256]{4,3,2,1,0:T(8,128)} %all-to-all-done.1.refs_0_, bf16[2,64,256]{2,1,0:T(8,128)(2,1)} %dynamic-slice_bitcast_fusion.3.refs_1_, f32[32,256,256]{2,1,0:T(8,128)} %depth_inverse.2.refs_2_), custom_call_target="tpu_custom_call" | custom-call | flops 805306368 | bytes 18874368 | tf_op jit(solution)/shard_map/depth_inverse/pallas_call | solution.py:145
  (50 shorter events, 32.6 us)
Async XLA Ops:
  13.8 6.5 copy-start.5
  13.8 63.7 %all-to-all-start.2 = ((f32[16,2,4,32,256]{4,3,2,1,0:T(8,128)}), f32[16,2,4,32,256]{4,3,2,1,0:T(8,128)}, u32[]{:S(2)}, u32[]{:S(2)}) async-start(f32[16,2,4,32,256]{4,3,2,1,0:T(8,128)} %depth_forward.3), calls=%async_computation.2 | async-start | bytes 8388608 | tf_op jit(solution)/shard_map/all_to_all | solution.py:326
  131.9 61.6 %all-to-all-start.6 = ((f32[16,2,4,32,256]{4,3,2,1,0:T(8,128)}), f32[16,2,4,32,256]{4,3,2,1,0:T(8,128)}, u32[]{:S(2)}, u32[]{:S(2)}) async-start(f32[16,2,4,32,256]{4,3,2,1,0:T(8,128)} %get-tuple-element.81), calls=%async_computation.6 | async-start | bytes 8388608 | tf_op jit(solution)/shard_map/all_to_all | solution.py:326
  136.4 6.2 copy-start.7
  193.5 115.4 %all-to-all-start.4 = ((f32[16,2,4,32,256]{4,3,2,1,0:T(8,128)}), f32[16,2,4,32,256]{4,3,2,1,0:T(8,128)}, u32[]{:S(2)}, u32[]{:S(2)}) async-start(f32[16,2,4,32,256]{4,3,2,1,0:T(8,128)} %scatter.16), calls=%async_computation.4 | async-start | bytes 8388608 | tf_op jit(solution)/shard_map/all_to_all | solution.py:326
  221.2 80.5 %collective-permute-start.3 = (f32[2,2,256,512]{3,2,1,0:T(8,128)}, f32[2,2,256,512]{3,2,1,0:T(8,128)S(1)}, u32[]{:S(2)}, u32[]{:S(2)}) collective-permute-start(f32[2,2,256,512]{3,2,1,0:T(8,128)} %get-tuple-element.77), channel_id=1, source_target_pairs={{0,12},{12,0},{1,13},{13,1},{2,14},{14,2},{3,15},{15,3},{16,28},{2... | collective-permute-start | bytes 6291464 | tf_op jit(solution)/shard_map/ppermute | solution.py:348
  226.9 74.8 %collective-permute-start.2 = (f32[2,2,256,512]{3,2,1,0:T(8,128)}, f32[2,2,256,512]{3,2,1,0:T(8,128)}, u32[]{:S(2)}, u32[]{:S(2)}) collective-permute-start(f32[2,2,256,512]{3,2,1,0:T(8,128)} %get-tuple-element.77), channel_id=1, source_target_pairs={{4,8},{8,4},{5,9},{9,5},{6,10},{10,6},{7,11},{11,7},{20,24},{24,20... | collective-permute-start | bytes 6291464 | tf_op jit(solution)/shard_map/ppermute | solution.py:347
  301.7 1.4 copy-start.3
  309.0 100.1 %all-to-all-start.3 = ((f32[16,2,2,32,256]{4,3,2,1,0:T(8,128)}), f32[16,2,2,32,256]{4,3,2,1,0:T(8,128)S(1)}, u32[]{:S(2)}, u32[]{:S(2)}) async-start(f32[16,2,2,32,256]{4,3,2,1,0:T(8,128)} %bitcast.32), calls=%async_computation.3 | async-start | bytes 4194304 | tf_op jit(solution)/shard_map/all_to_all | solution.py:326
  351.1 52.0 %collective-permute-start.7 = (f32[2,2,256,512]{3,2,1,0:T(8,128)}, f32[2,2,256,512]{3,2,1,0:T(8,128)}, u32[]{:S(2)}, u32[]{:S(2)}) collective-permute-start(f32[2,2,256,512]{3,2,1,0:T(8,128)} %get-tuple-element.83), channel_id=1, source_target_pairs={{0,12},{12,0},{1,13},{13,1},{2,14},{14,2},{3,15},{15,3},{16,28},{2... | collective-permute-start | bytes 6291464 | tf_op jit(solution)/shard_map/ppermute | solution.py:348
  356.0 47.1 %collective-permute-start.6 = (f32[2,2,256,512]{3,2,1,0:T(8,128)}, f32[2,2,256,512]{3,2,1,0:T(8,128)}, u32[]{:S(2)}, u32[]{:S(2)}) collective-permute-start(f32[2,2,256,512]{3,2,1,0:T(8,128)} %get-tuple-element.83), channel_id=1, source_target_pairs={{4,8},{8,4},{5,9},{9,5},{6,10},{10,6},{7,11},{11,7},{20,24},{24,20... | collective-permute-start | bytes 6291464 | tf_op jit(solution)/shard_map/ppermute | solution.py:347
  409.1 1.3 copy-start
  410.4 144.3 %all-to-all-start.7 = ((f32[16,2,2,32,256]{4,3,2,1,0:T(8,128)}), f32[16,2,2,32,256]{4,3,2,1,0:T(8,128)}, u32[]{:S(2)}, u32[]{:S(2)}) async-start(f32[16,2,2,32,256]{4,3,2,1,0:T(8,128)} %bitcast.31), calls=%async_computation.7 | async-start | bytes 4194304 | tf_op jit(solution)/shard_map/all_to_all | solution.py:326
  488.0 51.9 %collective-permute-start.5 = (f32[2,2,256,512]{3,2,1,0:T(8,128)}, f32[2,2,256,512]{3,2,1,0:T(8,128)S(1)}, u32[]{:S(2)}, u32[]{:S(2)}) collective-permute-start(f32[2,2,256,512]{3,2,1,0:T(8,128)} %scatter.19), channel_id=1, source_target_pairs={{0,12},{12,0},{1,13},{13,1},{2,14},{14,2},{3,15},{15,3},{16,28},{2... | collective-permute-start | bytes 6291464 | tf_op jit(solution)/shard_map/ppermute | solution.py:348
  493.4 47.6 %collective-permute-start.4 = (f32[2,2,256,512]{3,2,1,0:T(8,128)}, f32[2,2,256,512]{3,2,1,0:T(8,128)}, u32[]{:S(2)}, u32[]{:S(2)}) collective-permute-start(f32[2,2,256,512]{3,2,1,0:T(8,128)} %scatter.19), channel_id=1, source_target_pairs={{4,8},{8,4},{5,9},{9,5},{6,10},{10,6},{7,11},{11,7},{20,24},{24,20... | collective-permute-start | bytes 6291464 | tf_op jit(solution)/shard_map/ppermute | solution.py:347
  544.9 1.4 copy-start.2
  554.7 128.9 %all-to-all-start.5 = ((f32[16,2,2,32,256]{4,3,2,1,0:T(8,128)}), f32[16,2,2,32,256]{4,3,2,1,0:T(8,128)S(1)}, u32[]{:S(2)}, u32[]{:S(2)}) async-start(f32[16,2,2,32,256]{4,3,2,1,0:T(8,128)} %bitcast.30), calls=%async_computation.5 | async-start | bytes 4194304 | tf_op jit(solution)/shard_map/all_to_all | solution.py:326
  625.6 52.0 %collective-permute-start.1 = (f32[2,2,256,512]{3,2,1,0:T(8,128)}, f32[2,2,256,512]{3,2,1,0:T(8,128)}, u32[]{:S(2)}, u32[]{:S(2)}) collective-permute-start(f32[2,2,256,512]{3,2,1,0:T(8,128)} %get-tuple-element.75), channel_id=1, source_target_pairs={{0,12},{12,0},{1,13},{13,1},{2,14},{14,2},{3,15},{15,3},{16,28},{2... | collective-permute-start | bytes 6291464 | tf_op jit(solution)/shard_map/ppermute | solution.py:348
  630.2 47.4 %collective-permute-start = (f32[2,2,256,512]{3,2,1,0:T(8,128)}, f32[2,2,256,512]{3,2,1,0:T(8,128)}, u32[]{:S(2)}, u32[]{:S(2)}) collective-permute-start(f32[2,2,256,512]{3,2,1,0:T(8,128)} %get-tuple-element.75), channel_id=1, source_target_pairs={{4,8},{8,4},{5,9},{9,5},{6,10},{10,6},{7,11},{11,7},{20,24},{24,20... | collective-permute-start | bytes 6291464 | tf_op jit(solution)/shard_map/ppermute | solution.py:347
  683.6 50.3 %copy-start.1 = (f32[16,2,2,32,256]{4,3,2,1,0:T(8,128)}, f32[16,2,2,32,256]{4,3,2,1,0:T(8,128)S(1)}, u32[]{:S(2)}) copy-start(f32[16,2,2,32,256]{4,3,2,1,0:T(8,128)S(1)} %all-to-all-done.5.refs_1_) | copy-start | bytes 6291460
  683.6 49.0 %copy-start.6 = (bf16[2,2,64,256]{3,2,0,1:T(8,128)(2,1)S(1)}, bf16[2,2,64,256]{3,2,0,1:T(8,128)(2,1)}, u32[]{:S(2)}) copy-start(bf16[2,2,64,256]{3,2,0,1:T(8,128)(2,1)} %constant.206.clone) | copy-start | bytes 393220
  683.6 49.6 %copy-start.4 = (bf16[2,2,192,256]{3,2,0,1:T(8,128)(2,1)S(1)}, bf16[2,2,192,256]{3,2,0,1:T(8,128)(2,1)}, u32[]{:S(2)}) copy-start(bf16[2,2,192,256]{3,2,0,1:T(8,128)(2,1)} %constant.205.clone) | copy-start | bytes 1179652
  683.6 78.1 %all-to-all-start.1 = ((f32[16,2,2,32,256]{4,3,2,1,0:T(8,128)}), f32[16,2,2,32,256]{4,3,2,1,0:T(8,128)}, u32[]{:S(2)}, u32[]{:S(2)}) async-start(f32[16,2,2,32,256]{4,3,2,1,0:T(8,128)} %bitcast.33), calls=%async_computation.1 | async-start | bytes 4194304 | tf_op jit(solution)/shard_map/all_to_all | solution.py:326

commit v3 on v2

--- a/solution.py
+++ b/solution.py
@@ -232,14 +232,14 @@
     )(depth_index, wave_third, lines, *consts)
 
 
-def plane_inverse(own, near, far, tables_first, second):
+def plane_inverse(own, other, tables_first, second):
     count, _, rows, columns = own.shape
     columns //= 2
     others = rows // second
 
-    def kernel(own_ref, near_ref, far_ref, ir_ref, out_ref):
+    def kernel(own_ref, other_ref, ir_ref, out_ref):
         even, odd = (
-            dot3(split(own_ref[0, p] + (near_ref[0, p] + far_ref[0, p])), (ir_ref[0, p], ir_ref[1, p]))
+            dot3(split(own_ref[0, p] + other_ref[0, p]), (ir_ref[0, p], ir_ref[1, p]))
             for p in range(2)
         )
         for slab, value in enumerate((even + odd, even - odd)):
@@ -252,7 +252,7 @@
     return pl.pallas_call(
         kernel,
         grid=(count,),
-        in_specs=[spec, spec, spec, pl.BlockSpec(table.shape, lambda i: (0, 0, 0, 0))],
+        in_specs=[spec, spec, pl.BlockSpec(table.shape, lambda i: (0, 0, 0, 0))],
         out_specs=pl.BlockSpec((2, others, 1, 2, second, columns), lambda i: (0, 0, i, 0, 0, 0)),
         out_shape=jax.ShapeDtypeStruct((2, others, count, 2, second, columns), jnp.float32),
         compiler_params=pltpu.CompilerParams(vmem_limit_bytes=VMEM_LIMIT),
@@ -262,7 +262,7 @@
             transcendentals=0,
         ),
         name="plane_inverse",
-    )(own, near, far, table)
+    )(own, other, table)
 
 
 def wave_squares(length):
@@ -318,9 +318,7 @@
     scale = 1.0 / (total_first * total_second * depth)
 
     partners = [(i, others + (i ^ (others // 2))) for i in range(others)]
-    both_ways = [((a, b), (b, a)) for a, b in partners]
-    far_pairs = [pair for way in both_ways[: others // 2] for pair in way]
-    near_pairs = [pair for way in both_ways[others // 2 :] for pair in way]
+    pairs = [pair for a, b in partners for pair in ((a, b), (b, a))]
 
     def exchange(value):
         return lax.all_to_all(value, group, split_axis=0, concat_axis=0, tiled=True)
@@ -344,13 +342,11 @@
         if chunk == zero_chunk:
             spot = (0, 0, 0, first)
             other = other.at[spot].set(jnp.where(is_zero, mass, other[spot]))
-        near = lax.ppermute(other, ("half", "other"), near_pairs)
-        far = lax.ppermute(other, ("half", "other"), far_pairs)
+        other = lax.ppermute(other, ("half", "other"), pairs)
         if chunk == zero_chunk:
-            mass += near[spot] + far[spot]
-            near = near.at[spot].set(jnp.where(is_zero, 0.0, near[spot]))
-            far = far.at[spot].set(jnp.where(is_zero, 0.0, far[spot]))
-        fresh = plane_inverse(own, near, far, tables_first, second)
+            mass += other[spot]
+            other = other.at[spot].set(jnp.where(is_zero, 0.0, other[spot]))
+        fresh = plane_inverse(own, other, tables_first, second)
         if chunk == zero_chunk:
             spot = (slice(None), slice(None), 0, 1, 0, 0)
             fresh = fresh.at[spot].set(jnp.where(is_zero, mass, fresh[spot]))

time: 779 us -> 765 us (0.982)
  starting transfers between devices: 208 us -> 187 us
  waiting for transfers between devices: 305 us -> 319 us
    ppermute x8 -> x4, starting transfers between devices: 28.7 us -> 10.9 us  [local(): other = lax.ppermute(other, ('half', 'other'), pairs)]
    ppermute x8 -> x4, waiting for transfers between devices: 208 us -> 221 us  [local(): other = lax.ppermute(other, ('half', 'other'), pairs)]
  transfers between devices with their start and end apart: 15 -> 11, of which waited for: 7 -> 7; matrix products, arithmetic and copies ran while one was open for 3% -> 3% of each run, Pallas kernels for 19% -> 19%
where the time goes in v3:
time: 765 us; the launch traced here: 763 us
  waiting for transfers between devices  319 us (42%)
  starting transfers between devices  187 us (24%)
  Pallas kernels  171 us (22%)
  blocking collectives  54.4 us (7%)
  other arithmetic  14.7 us (2%)
  local copies, waits for them, and re-layouts  14.1 us (2%)
    ppermute x4, waiting for transfers between devices, local(): other = lax.ppermute(other, ('half', 'other'), pairs)  221 us
    all_to_all x7, starting transfers between devices, exchange(): return lax.all_to_all(value, group, split_axis=0, concat_axis=0, tiled=True)  176 us
    all_to_all x7, waiting for transfers between devices, exchange(): return lax.all_to_all(value, group, split_axis=0, concat_axis=0, tiled=True)  97.9 us
    pallas_call x4, Pallas kernels, plane_forward(): pl.pallas_call(kernel, grid=(count,), in_specs=[smem, smem, pl.BlockSpec(...  90.5 us
    all_to_all x1, blocking collectives, exchange(): return lax.all_to_all(value, group, split_axis=0, concat_axis=0, tiled=True)  54.4 us
    pallas_call x2, Pallas kernels, depth_forward(): pl.pallas_call(kernel, grid=(second // 8, first // LANES), in_specs=[pl.B...  33 us
    pallas_call x2, Pallas kernels, depth_inverse(): pl.pallas_call(kernel, grid=(second // 8, first // LANES, depth // width)...  26.1 us
    pallas_call x4, Pallas kernels, plane_inverse(): pl.pallas_call(kernel, grid=(count,), in_specs=[spec, spec, pl.BlockSpec(...  21.1 us
  transfers between devices with their start and end apart: 11, of which 7 were waited for; matrix products, arithmetic and copies ran while one was open for 3% of the time, Pallas kernels for 19%

profile of v3, /device:TPU:0, one launch (start us, length us, event | category | flops | bytes accessed | tf_op | source)
XLA Modules:
  0.0 763.1 jit_solution(899472745908719244)
XLA Ops:
  2.1 11.7 %depth_forward.3 = f32[16,2,4,32,256]{4,3,2,1,0:T(8,128)} custom-call(f32[256,32,256]{2,1,0:T(8,128)} %refs_1_.3, f32[256,32,256]{2,1,0:T(8,128)} %refs_1_.3, bf16[2,64,256]{2,1,0:T(8,128)(2,1)} %dynamic-slice_bitcast_fusion.2.refs_2_), custom_call_target="tpu_custom_call" | custom-call | flops 1610612736 | bytes 12582912 | tf_op jit(solution)/shard_map/depth_forward/pallas_call | solution.py:93
  13.8 6.5 all-to-all-start.2
  21.0 21.3 %depth_forward.2 = (f32[16,2,4,32,256]{4,3,2,1,0:T(8,128)}, f32[16,2,4,32,256]{4,3,2,1,0:T(8,128)}, f32[16,2,4,32,256]{4,3,2,1,0:T(8,128)}) custom-call(f32[256,32,256]{2,1,0:T(8,128)} %refs_1_.3, f32[256,32,256]{2,1,0:T(8,128)} %refs_1_.3, bf16[2,192,256]{2,1,0:T(8,128)(2,1)} %dynamic-slice_bitcast_fusion.1.refs_2_), custom_call_target="tpu_custom_call" | custom-call | flops 4831838208 | bytes 20971520 | tf_op jit(solution)/shard_map/depth_forward/pallas_call | solution.py:93
  42.3 35.2 %all-to-all-done.2 = f32[16,2,4,32,256]{4,3,2,1,0:T(8,128)} async-done(((f32[16,2,4,32,256]{4,3,2,1,0:T(8,128)}), f32[16,2,4,32,256]{4,3,2,1,0:T(8,128)}, u32[]{:S(2)}, u32[]{:S(2)}) %all-to-all-start.2) | async-done | bytes 4194336 | tf_op jit(solution)/shard_map/all_to_all | solution.py:324
  77.5 54.4 %all_to_all.40 = f32[16,2,4,32,256]{4,3,2,1,0:T(8,128)} all-to-all(f32[16,2,4,32,256]{4,3,2,1,0:T(8,128)} %get-tuple-element.61), channel_id=1, replica_groups=mesh['slab'=2,'half'=2,'other'=8] {'slab','other'}, dimensions={0} | all-to-all | bytes 8388608 | tf_op jit(solution)/shard_map/all_to_all | solution.py:324
  131.9 4.6 all-to-all-start.6
  136.4 6.2 reduce_sum.18
  143.3 2.5 fusion
  147.7 45.8 %all-to-all-done.6 = f32[16,2,4,32,256]{4,3,2,1,0:T(8,128)} async-done(((f32[16,2,4,32,256]{4,3,2,1,0:T(8,128)}), f32[16,2,4,32,256]{4,3,2,1,0:T(8,128)}, u32[]{:S(2)}, u32[]{:S(2)}) %all-to-all-start.6) | async-done | bytes 4194336 | tf_op jit(solution)/shard_map/all_to_all | solution.py:324
  193.5 4.6 all-to-all-start.4
  198.8 22.5 %plane_forward.5 = (f32[2,2,256,512]{3,2,1,0:T(8,128)}, f32[2,2,256,512]{3,2,1,0:T(8,128)}) custom-call(s32[2]{0:T(128)} %pad_add_fusion.2.index_ref, f32[128]{0:T(128)} %constant.184.clone.third_ref, f32[2,8,2,4,32,256]{5,4,3,2,1,0:T(8,128)} %bitcast.7.lines_ref, f32[2,256]{1,0:T(2,128)} %constant.182.clone.wf_ref, f32[2,256,1]{2,1,0:T(8,128)} %constant.183.clone.ws_ref, ...), custom_call_target="tpu_custom_call" | custom-call | flops 12884901888 | bytes 8388608 | tf_op jit(solution)/shard_map/plane_forward/pallas_call | solution.py:217
  221.3 3.8 collective-permute-start.1
  225.1 76.6 %collective-permute-done.1.other_ref = f32[2,2,256,512]{3,2,1,0:T(8,128)S(1)} collective-permute-done((f32[2,2,256,512]{3,2,1,0:T(8,128)}, f32[2,2,256,512]{3,2,1,0:T(8,128)S(1)}, u32[]{:S(2)}, u32[]{:S(2)}) %collective-permute-start.1) | collective-permute-done | bytes 2097184 | tf_op jit(solution)/shard_map/ppermute | solution.py:345
  303.0 5.3 plane_inverse.5
  308.3 17.4 %all-to-all-start.3 = ((f32[16,2,2,32,256]{4,3,2,1,0:T(8,128)}), f32[16,2,2,32,256]{4,3,2,1,0:T(8,128)S(1)}, u32[]{:S(2)}, u32[]{:S(2)}) async-start(f32[16,2,2,32,256]{4,3,2,1,0:T(8,128)} %bitcast.30), calls=%async_computation.3 | async-start | bytes 4194304 | tf_op jit(solution)/shard_map/all_to_all | solution.py:324
  326.3 22.7 %plane_forward.7 = (f32[2,2,256,512]{3,2,1,0:T(8,128)}, f32[2,2,256,512]{3,2,1,0:T(8,128)}) custom-call(s32[2]{0:T(128)} %pad_add_fusion.index_ref, f32[128]{0:T(128)} %constant.184.clone.third_ref, f32[2,8,2,4,32,256]{5,4,3,2,1,0:T(8,128)} %bitcast.20.lines_ref, f32[2,256]{1,0:T(2,128)} %constant.182.clone.wf_ref, f32[2,256,1]{2,1,0:T(8,128)} %constant.183.clone.ws_ref, ...), custom_call_target="tpu_custom_call" | custom-call | flops 12884901888 | bytes 8388608 | tf_op jit(solution)/shard_map/plane_forward/pallas_call | solution.py:217
  349.0 3.0 collective-permute-start.3
  352.0 48.3 %collective-permute-done.3.other_ref = f32[2,2,256,512]{3,2,1,0:T(8,128)} collective-permute-done((f32[2,2,256,512]{3,2,1,0:T(8,128)}, f32[2,2,256,512]{3,2,1,0:T(8,128)}, u32[]{:S(2)}, u32[]{:S(2)}) %collective-permute-start.3) | collective-permute-done | bytes 2097184 | tf_op jit(solution)/shard_map/ppermute | solution.py:345
  400.3 5.3 plane_inverse.7
  406.9 46.8 %all-to-all-start.7 = ((f32[16,2,2,32,256]{4,3,2,1,0:T(8,128)}), f32[16,2,2,32,256]{4,3,2,1,0:T(8,128)}, u32[]{:S(2)}, u32[]{:S(2)}) async-start(f32[16,2,2,32,256]{4,3,2,1,0:T(8,128)} %bitcast.29), calls=%async_computation.7 | async-start | bytes 4194304 | tf_op jit(solution)/shard_map/all_to_all | solution.py:324
  454.3 22.7 %plane_forward.6 = (f32[2,2,256,512]{3,2,1,0:T(8,128)}, f32[2,2,256,512]{3,2,1,0:T(8,128)}) custom-call(s32[2]{0:T(128)} %pad_add_fusion.1.index_ref, f32[128]{0:T(128)} %constant.184.clone.third_ref, f32[2,8,2,4,32,256]{5,4,3,2,1,0:T(8,128)} %bitcast.13.lines_ref, f32[2,256]{1,0:T(2,128)} %constant.182.clone.wf_ref, f32[2,256,1]{2,1,0:T(8,128)} %constant.183.clone.ws_ref, ...), custom_call_target="tpu_custom_call" | custom-call | flops 12884901888 | bytes 8388608 | tf_op jit(solution)/shard_map/plane_forward/pallas_call | solution.py:217
  482.2 2.4 collective-permute-start.2
  484.6 47.6 %collective-permute-done.2 = f32[2,2,256,512]{3,2,1,0:T(8,128)S(1)} collective-permute-done((f32[2,2,256,512]{3,2,1,0:T(8,128)}, f32[2,2,256,512]{3,2,1,0:T(8,128)S(1)}, u32[]{:S(2)}, u32[]{:S(2)}) %collective-permute-start.2) | collective-permute-done | bytes 2097184 | tf_op jit(solution)/shard_map/ppermute | solution.py:345
  535.9 5.3 plane_inverse.6
  543.5 47.9 %all-to-all-start.5 = ((f32[16,2,2,32,256]{4,3,2,1,0:T(8,128)}), f32[16,2,2,32,256]{4,3,2,1,0:T(8,128)S(1)}, u32[]{:S(2)}, u32[]{:S(2)}) async-start(f32[16,2,2,32,256]{4,3,2,1,0:T(8,128)} %bitcast.28), calls=%async_computation.5 | async-start | bytes 4194304 | tf_op jit(solution)/shard_map/all_to_all | solution.py:324
  592.1 22.7 %plane_forward.4 = (f32[2,2,256,512]{3,2,1,0:T(8,128)}, f32[2,2,256,512]{3,2,1,0:T(8,128)}) custom-call(s32[2]{0:T(128)} %pad_add_fusion.3.index_ref, f32[128]{0:T(128)} %constant.184.clone.third_ref, f32[2,8,2,4,32,256]{5,4,3,2,1,0:T(8,128)} %bitcast.32, f32[2,256]{1,0:T(2,128)} %constant.182.clone.wf_ref, f32[2,256,1]{2,1,0:T(8,128)} %constant.183.clone.ws_ref, ...), custom_call_target="tpu_custom_call" | custom-call | flops 12884901888 | bytes 8388608 | tf_op jit(solution)/shard_map/plane_forward/pallas_call | solution.py:217
  616.4 48.5 %collective-permute-done.other_ref = f32[2,2,256,512]{3,2,1,0:T(8,128)} collective-permute-done((f32[2,2,256,512]{3,2,1,0:T(8,128)}, f32[2,2,256,512]{3,2,1,0:T(8,128)}, u32[]{:S(2)}, u32[]{:S(2)}) %collective-permute-start) | collective-permute-done | bytes 2097184 | tf_op jit(solution)/shard_map/ppermute | solution.py:345
  664.9 5.3 plane_inverse.4
  670.2 48.1 %all-to-all-start.1 = ((f32[16,2,2,32,256]{4,3,2,1,0:T(8,128)}), f32[16,2,2,32,256]{4,3,2,1,0:T(8,128)}, u32[]{:S(2)}, u32[]{:S(2)}) async-start(f32[16,2,2,32,256]{4,3,2,1,0:T(8,128)} %bitcast.31), calls=%async_computation.1 | async-start | bytes 4194304 | tf_op jit(solution)/shard_map/all_to_all | solution.py:324
  720.1 10.3 %depth_inverse.2.refs_2_ = f32[32,256,256]{2,1,0:T(8,128)} custom-call(f32[16,2,2,32,256]{4,3,2,1,0:T(8,128)} %copy-done, f32[16,2,2,32,256]{4,3,2,1,0:T(8,128)} %copy-done.1, f32[16,2,2,32,256]{4,3,2,1,0:T(8,128)} %all-to-all-done.7.refs_2_, bf16[2,192,256]{2,1,0:T(8,128)(2,1)} %dynamic-slice_bitcast_fusion.refs_3_), custom_call_target="tpu_custom_call" | custom-call | flops 2415919104 | bytes 14680064 | tf_op jit(solution)/shard_map/depth_inverse/pallas_call | solution.py:145
  730.4 16.9 %all-to-all-done.1.refs_0_ = f32[16,2,2,32,256]{4,3,2,1,0:T(8,128)} async-done(((f32[16,2,2,32,256]{4,3,2,1,0:T(8,128)}), f32[16,2,2,32,256]{4,3,2,1,0:T(8,128)}, u32[]{:S(2)}, u32[]{:S(2)}) %all-to-all-start.1) | async-done | bytes 2097184 | tf_op jit(solution)/shard_map/all_to_all | solution.py:324
  747.4 15.7 %depth_inverse.3 = f32[256,32,256]{2,1,0:T(8,128)} custom-call(f32[16,2,2,32,256]{4,3,2,1,0:T(8,128)} %all-to-all-done.1.refs_0_, bf16[2,64,256]{2,1,0:T(8,128)(2,1)} %dynamic-slice_bitcast_fusion.3.refs_1_, f32[32,256,256]{2,1,0:T(8,128)} %depth_inverse.2.refs_2_), custom_call_target="tpu_custom_call" | custom-call | flops 805306368 | bytes 18874368 | tf_op jit(solution)/shard_map/depth_inverse/pallas_call | solution.py:145
  (40 shorter events, 21.8 us)
Async XLA Ops:
  13.8 6.5 copy-start.5
  13.8 63.7 %all-to-all-start.2 = ((f32[16,2,4,32,256]{4,3,2,1,0:T(8,128)}), f32[16,2,4,32,256]{4,3,2,1,0:T(8,128)}, u32[]{:S(2)}, u32[]{:S(2)}) async-start(f32[16,2,4,32,256]{4,3,2,1,0:T(8,128)} %depth_forward.3), calls=%async_computation.2 | async-start | bytes 8388608 | tf_op jit(solution)/shard_map/all_to_all | solution.py:324
  131.9 61.6 %all-to-all-start.6 = ((f32[16,2,4,32,256]{4,3,2,1,0:T(8,128)}), f32[16,2,4,32,256]{4,3,2,1,0:T(8,128)}, u32[]{:S(2)}, u32[]{:S(2)}) async-start(f32[16,2,4,32,256]{4,3,2,1,0:T(8,128)} %get-tuple-element.69), calls=%async_computation.6 | async-start | bytes 8388608 | tf_op jit(solution)/shard_map/all_to_all | solution.py:324
  136.4 6.2 copy-start.7
  193.5 114.8 %all-to-all-start.4 = ((f32[16,2,4,32,256]{4,3,2,1,0:T(8,128)}), f32[16,2,4,32,256]{4,3,2,1,0:T(8,128)}, u32[]{:S(2)}, u32[]{:S(2)}) async-start(f32[16,2,4,32,256]{4,3,2,1,0:T(8,128)} %scatter.14), calls=%async_computation.4 | async-start | bytes 8388608 | tf_op jit(solution)/shard_map/all_to_all | solution.py:324
  221.3 80.4 %collective-permute-start.1 = (f32[2,2,256,512]{3,2,1,0:T(8,128)}, f32[2,2,256,512]{3,2,1,0:T(8,128)S(1)}, u32[]{:S(2)}, u32[]{:S(2)}) collective-permute-start(f32[2,2,256,512]{3,2,1,0:T(8,128)} %get-tuple-element.65), channel_id=1, source_target_pairs={{0,12},{12,0},{1,13},{13,1},{2,14},{14,2},{3,15},{15,3},{4,8},{8,4... | collective-permute-start | bytes 6291464 | tf_op jit(solution)/shard_map/ppermute | solution.py:345
  301.7 1.3 copy-start.3
  308.3 97.3 %all-to-all-start.3 = ((f32[16,2,2,32,256]{4,3,2,1,0:T(8,128)}), f32[16,2,2,32,256]{4,3,2,1,0:T(8,128)S(1)}, u32[]{:S(2)}, u32[]{:S(2)}) async-start(f32[16,2,2,32,256]{4,3,2,1,0:T(8,128)} %bitcast.30), calls=%async_computation.3 | async-start | bytes 4194304 | tf_op jit(solution)/shard_map/all_to_all | solution.py:324
  349.0 51.3 %collective-permute-start.3 = (f32[2,2,256,512]{3,2,1,0:T(8,128)}, f32[2,2,256,512]{3,2,1,0:T(8,128)}, u32[]{:S(2)}, u32[]{:S(2)}) collective-permute-start(f32[2,2,256,512]{3,2,1,0:T(8,128)} %get-tuple-element.71), channel_id=1, source_target_pairs={{0,12},{12,0},{1,13},{13,1},{2,14},{14,2},{3,15},{15,3},{4,8},{8,4... | collective-permute-start | bytes 6291464 | tf_op jit(solution)/shard_map/ppermute | solution.py:345
  405.5 1.3 copy-start
  406.9 136.7 %all-to-all-start.7 = ((f32[16,2,2,32,256]{4,3,2,1,0:T(8,128)}), f32[16,2,2,32,256]{4,3,2,1,0:T(8,128)}, u32[]{:S(2)}, u32[]{:S(2)}) async-start(f32[16,2,2,32,256]{4,3,2,1,0:T(8,128)} %bitcast.29), calls=%async_computation.7 | async-start | bytes 4194304 | tf_op jit(solution)/shard_map/all_to_all | solution.py:324
  482.2 50.0 %collective-permute-start.2 = (f32[2,2,256,512]{3,2,1,0:T(8,128)}, f32[2,2,256,512]{3,2,1,0:T(8,128)S(1)}, u32[]{:S(2)}, u32[]{:S(2)}) collective-permute-start(f32[2,2,256,512]{3,2,1,0:T(8,128)} %scatter.15), channel_id=1, source_target_pairs={{0,12},{12,0},{1,13},{13,1},{2,14},{14,2},{3,15},{15,3},{4,8},{8,4... | collective-permute-start | bytes 6291464 | tf_op jit(solution)/shard_map/ppermute | solution.py:345
  534.5 1.3 copy-start.2
  543.5 126.6 %all-to-all-start.5 = ((f32[16,2,2,32,256]{4,3,2,1,0:T(8,128)}), f32[16,2,2,32,256]{4,3,2,1,0:T(8,128)S(1)}, u32[]{:S(2)}, u32[]{:S(2)}) async-start(f32[16,2,2,32,256]{4,3,2,1,0:T(8,128)} %bitcast.28), calls=%async_computation.5 | async-start | bytes 4194304 | tf_op jit(solution)/shard_map/all_to_all | solution.py:324
  614.7 50.1 %collective-permute-start = (f32[2,2,256,512]{3,2,1,0:T(8,128)}, f32[2,2,256,512]{3,2,1,0:T(8,128)}, u32[]{:S(2)}, u32[]{:S(2)}) collective-permute-start(f32[2,2,256,512]{3,2,1,0:T(8,128)} %get-tuple-element.63), channel_id=1, source_target_pairs={{0,12},{12,0},{1,13},{13,1},{2,14},{14,2},{3,15},{15,3},{4,8},{8,4... | collective-permute-start | bytes 6291464 | tf_op jit(solution)/shard_map/ppermute | solution.py:345
  670.2 49.4 %copy-start.1 = (f32[16,2,2,32,256]{4,3,2,1,0:T(8,128)}, f32[16,2,2,32,256]{4,3,2,1,0:T(8,128)S(1)}, u32[]{:S(2)}) copy-start(f32[16,2,2,32,256]{4,3,2,1,0:T(8,128)S(1)} %all-to-all-done.5.refs_1_) | copy-start | bytes 6291460
  670.2 48.1 %copy-start.6 = (bf16[2,2,64,256]{3,2,0,1:T(8,128)(2,1)S(1)}, bf16[2,2,64,256]{3,2,0,1:T(8,128)(2,1)}, u32[]{:S(2)}) copy-start(bf16[2,2,64,256]{3,2,0,1:T(8,128)(2,1)} %constant.188.clone) | copy-start | bytes 393220
  670.2 48.7 %copy-start.4 = (bf16[2,2,192,256]{3,2,0,1:T(8,128)(2,1)S(1)}, bf16[2,2,192,256]{3,2,0,1:T(8,128)(2,1)}, u32[]{:S(2)}) copy-start(bf16[2,2,192,256]{3,2,0,1:T(8,128)(2,1)} %constant.187.clone) | copy-start | bytes 1179652
  670.2 77.2 %all-to-all-start.1 = ((f32[16,2,2,32,256]{4,3,2,1,0:T(8,128)}), f32[16,2,2,32,256]{4,3,2,1,0:T(8,128)}, u32[]{:S(2)}, u32[]{:S(2)}) async-start(f32[16,2,2,32,256]{4,3,2,1,0:T(8,128)} %bitcast.31), calls=%async_computation.1 | async-start | bytes 4194304 | tf_op jit(solution)/shard_map/all_to_all | solution.py:324
